TPU v7x, 256 devices: a whole 4x4x8 slice. The times are simulated.
256 devices in a mesh: row: 16 (over y_hi, x, core), col: 16 (over z, y_lo).
Axes of the slice: x: 4, y: 4 (y_hi: 2, y_lo: 2; y = y_hi * 2 + y_lo), z: 8, core: 2. Of those that a mesh axis runs over, the one named last changes fastest.
Arguments:
- trailing: float32 [12288, 16384], P('row', 'col'), may hold values from -6 to 6
- column_block: bfloat16 [12288, 1024], P('row', 'col'), may hold values from -6 to 6
- row_block: bfloat16 [1024, 16384], P('row', 'col'), may hold values from -0.1875 to 0.1875
- lower_inv: bfloat16 [1024, 1024], replicated, may hold values from -1 to 1, as said below
- upper_inv: bfloat16 [1024, 1024], replicated, may hold values from -2 to 2, as said below
Outputs:
- lower_panel: bfloat16 [12288, 1024], P('row', 'col')
- upper_panel: bfloat16 [1024, 16384], P('row', 'col')
- updated: float32 [12288, 16384], P('row', 'col')
Inputs may be any that keep to these rules, and one draw needn't show every extreme that they name: `lower_inv`: lower triangular with ones on the diagonal. `upper_inv`: upper triangular with diagonal entries between 0.5 and 2.
All inputs are finite; a program needn't handle non-finite values.
Results may differ from a plain program's by a relative error of at most 0.0044.
Values may be sent and summed in bfloat16 or wider, within the bound.
No kernel may reach another device: no remote copies, remote signals or barrier semaphores. Data moves between devices by JAX's collectives and lax.ppermute only.
A program may use at most 64 MiB of HBM per device.

v0:
```python
import jax
import jax.numpy as jnp
from jax import lax
from jax.sharding import PartitionSpec as P


def on_device(trailing, column_block, row_block, lower_inv, upper_inv):
    col_share = column_block.shape[1]
    row_share = row_block.shape[0]
    col_start = lax.axis_index("col") * col_share
    row_start = lax.axis_index("row") * row_share
    factor = upper_inv
    lower_full = jnp.dot(
        lax.all_gather(column_block, "col", axis=1, tiled=True),
        factor,
        preferred_element_type=jnp.float32,
    ).astype(jnp.bfloat16)
    factor = lower_inv
    upper_full = jnp.dot(
        factor,
        lax.all_gather(row_block, "row", axis=0, tiled=True),
        preferred_element_type=jnp.float32,
    ).astype(jnp.bfloat16)
    product = jnp.dot(lower_full, upper_full, preferred_element_type=jnp.float32)
    lower_tile = lax.dynamic_slice_in_dim(lower_full, col_start, col_share, 1)
    upper_tile = lax.dynamic_slice_in_dim(upper_full, row_start, row_share, 0)
    updated = trailing - product
    return (lower_tile, upper_tile, updated)


def solution(mesh):
    in_specs = (P("row", "col"), P("row", "col"), P("row", "col"), P(), P())
    out_specs = (P("row", "col"), P("row", "col"), P("row", "col"))
    return jax.shard_map(
        on_device, mesh=mesh, in_specs=in_specs, out_specs=out_specs, check_vma=False
    )
```

profile of v0, /device:TPU:1, one launch (start us, length us, event | category | flops | bytes accessed | tf_op | source)
XLA Modules:
  0.0 155.6 jit_solution(6952188676541662737)
XLA Ops:
  7.2 0.0 copy-start
  7.2 0.0 all-gather.3.cloned.1.call-start
  7.2 0.7 all-gather.3.cloned.1.call-update
  7.9 0.0 all-gather.5.cloned.1.call-start
  8.0 0.7 all-gather.5.cloned.1.call-update
  8.7 66.0 %all-gather.3.cloned.1.call-done = bf16[768,1024]{0,1:T(8,128)(2,1)} async-done(((bf16[768,64]{0,1:T(8,128)(2,1)}), bf16[768,1024]{0,1:T(8,128)(2,1)}) %all-gather.3.cloned.1.call-update) | async-done | bytes 1572880 | tf_op jit(solution)/shard_map/all_gather | solution.py:14
  74.6 3.9 %convolution_convert_fusion.1 = bf16[768,1024]{1,0:T(8,128)(2,1)S(1)} fusion(bf16[768,1024]{0,1:T(8,128)(2,1)} %all-gather.3.cloned.1.call-done, bf16[1024,1024]{1,0:T(8,128)(2,1)} %param.9), kind=kOutput, calls=%fused_computation.2 | convolution fusion | flops 1611399168 | bytes 5242880 | tf_op jit(solution)/shard_map/dot_general | solution.py:13
  78.5 0.0 copy-start.1
  78.5 1.1 copy-done.1
  79.7 0.1 constant_dynamic-slice_fusion.1
  79.8 0.8 copy.8
  80.6 60.0 %all-gather.5.cloned.1.call-done = bf16[1024,1024]{1,0:T(8,128)(2,1)} async-done(((bf16[64,1024]{1,0:T(8,128)(2,1)}), bf16[1024,1024]{1,0:T(8,128)(2,1)}) %all-gather.5.cloned.1.call-update) | async-done | bytes 2097168 | tf_op jit(solution)/shard_map/all_gather | solution.py:21
  140.5 0.0 copy-done
  140.5 0.0 copy-start.2
  140.5 0.0 copy-start.3
  140.5 4.1 %convolution_convert_fusion = bf16[1024,1024]{1,0:T(8,128)(2,1)S(1)} fusion(bf16[1024,1024]{1,0:T(8,128)(2,1)S(1)} %copy-done, bf16[1024,1024]{1,0:T(8,128)(2,1)} %all-gather.5.cloned.1.call-done), kind=kOutput, calls=%fused_computation | convolution fusion | flops 2148532224 | bytes 6291456 | tf_op jit(solution)/shard_map/dot_general | solution.py:19
  144.6 0.7 constant_dynamic-slice_fusion
  145.3 0.0 copy-done.2
  145.3 0.0 copy-done.3
  145.3 3.5 %convolution_subtract_fusion = f32[768,1024]{1,0:T(8,128)} fusion(f32[768,1024]{1,0:T(8,128)S(1)} %copy-done.3, bf16[768,1024]{1,0:T(8,128)(2,1)S(1)} %copy-done.2, bf16[1024,1024]{1,0:T(8,128)(2,1)S(1)} %convolution_convert_fusion), kind=kOutput, calls=%fused_computation.1 | convolution fusion | flops 1611399168 | bytes 9961472 | tf_op jit(solution)/shard_map/dot_general | solution.py:24
Async XLA Ops:
  7.2 133.4 %copy-start = (bf16[1024,1024]{1,0:T(8,128)(2,1)S(1)}, bf16[1024,1024]{1,0:T(8,128)(2,1)}, u32[]{:S(2)}) copy-start(bf16[1024,1024]{1,0:T(8,128)(2,1)} %param.8) | copy-start | bytes 6291460
  7.2 67.4 %all-gather.3.cloned.1.call-start = ((), (), s32[]{:S(2)}) async-start(), calls=%async_computation | async-start | bytes 1671168 | tf_op jit(solution)/shard_map/all_gather | solution.py:14
  7.9 132.6 %all-gather.5.cloned.1.call-start = ((), (), s32[]{:S(2)}) async-start(), calls=%async_computation.1 | async-start | bytes 2228224 | tf_op jit(solution)/shard_map/all_gather | solution.py:21
  78.5 1.1 copy-start.1
  140.5 4.8 %copy-start.2 = (bf16[768,1024]{1,0:T(8,128)(2,1)S(1)}, bf16[768,1024]{1,0:T(8,128)(2,1)}, u32[]{:S(2)}) copy-start(bf16[768,1024]{1,0:T(8,128)(2,1)} %copy-done.1) | copy-start | bytes 4718596
  140.5 4.8 %copy-start.3 = (f32[768,1024]{1,0:T(8,128)S(1)}, f32[768,1024]{1,0:T(8,128)}, u32[]{:S(2)}) copy-start(f32[768,1024]{1,0:T(8,128)} %param.5) | copy-start | bytes 9437188
Sparse Core Ops, SparseCore 0:
  9.8 64.7 all-gather.2
  77.4 63.1 all-gather.4
where the time goes:
time: 156 us
  waiting for transfers between devices  127 us (81%)
  between operations  14.1 us (9%)
  matrix products  11.4 us (7%)
  local copies, waits for them, and re-layouts  2.73 us (2%)
    all_gather x1, waiting for transfers between devices, on_device(): lax.all_gather(column_block, 'col', axis=1, tiled=True)  66 us
    all_gather x1, waiting for transfers between devices, on_device(): lax.all_gather(row_block, 'row', axis=0, tiled=True)  60 us
    dot_general x1, matrix products, on_device(): jnp.dot(factor, lax.all_gather(row_block, 'row', axis=0, tiled=True), pre...  4.06 us
    dot_general x1, matrix products, on_device(): jnp.dot(lax.all_gather(column_block, 'col', axis=1, tiled=True), factor,...  3.89 us
    dot_general x1, matrix products, on_device(): jnp.dot(lower_full, upper_full, preferred_element_type=jnp.float32)  3.47 us
  transfers between devices with their start and end apart: 2, of which 2 were waited for; matrix products, arithmetic and copies ran while one was open for 3% of the time, Pallas kernels for 0%

commit v1 on v0

v1 whole, which is shorter than its diff:
```python
import jax
import jax.numpy as jnp
from jax import lax
from jax.sharding import PartitionSpec as P


def split(row, col):
    return row >> 3, (row >> 1) & 3, row & 1, col >> 1, col & 1


def pairs_of(rows, cols, target):
    pairs = []
    for row in range(rows):
        for col in range(cols):
            half, x, core, z, low = target(*split(row, col))
            to_row = ((half % 2) * 4 + x % 4) * 2 + core
            to_col = (z % 8) * 2 + low
            pairs.append((row * cols + col, to_row * cols + to_col))
    return pairs


def on_device(trailing, column_block, row_block, lower_inv, upper_inv):
    def send(block, target):
        return lax.ppermute(block, ("row", "col"), pairs_of(16, 16, target))

    def from_z(block, step):
        return send(block, lambda half, x, core, z, low: (half, x, core, z - step, low))

    def from_x(block, step):
        return send(block, lambda half, x, core, z, low: (half, x - step, core, z, low))

    def from_half(block):
        return send(block, lambda half, x, core, z, low: (half ^ 1, x, core, z, low))

    def from_low(block):
        return send(block, lambda half, x, core, z, low: (half, x, core, z, low ^ 1))

    def from_core(block):
        return send(block, lambda half, x, core, z, low: (half, x, core ^ 1, z, low))

    row, col = lax.axis_index("row"), lax.axis_index("col")
    half, x, core, z, low = split(row, col)
    share = column_block.shape[1]
    own_a, own_b = column_block.T, row_block

    other_half = from_half(own_b)
    other_low = from_low(own_a)
    a_next, a_prev, a_far = from_z(own_a, 1), from_z(own_a, -1), from_z(own_a, 4)

    b_two = jnp.concatenate([own_b, other_half], 0)
    b_x = [b_two, from_x(b_two, 1), from_x(b_two, 2), from_x(b_two, 3)]
    b_mine = jnp.concatenate(b_x, 0)
    b_theirs = from_core(b_mine)

    three = jnp.concatenate([a_next, a_far, a_prev], 0)
    up = from_z(three[: 2 * share], 1)
    down = from_z(three[share:], -1)
    low_three = from_low(three)
    low_up = from_z(low_three[: 2 * share], 1)
    low_down = from_z(low_three[share:], -1)

    def part(block, index):
        return block[index * share : (index + 1) * share]

    mine = [own_a, a_next, part(up, 0), part(down, 0), a_far, part(up, 1), part(down, 1), a_prev]
    theirs = [
        other_low, part(low_three, 0), part(low_up, 0), part(low_down, 0),
        part(low_three, 1), part(low_up, 1), part(low_down, 1), part(low_three, 2),
    ]
    mine[3], mine[6] = part(down, 0), part(down, 1)
    theirs[3], theirs[6] = part(low_down, 0), part(low_down, 1)
    a_all = jnp.concatenate(mine + theirs, 0)

    nb = upper_inv.shape[0]
    width = nb // 8
    turned = lax.dynamic_slice_in_dim(jnp.concatenate([upper_inv, upper_inv], 0), z * width, nb, 0)
    turned = turned.reshape(8, 2, share, nb)
    turned = jnp.where(low == 0, turned, turned[:, ::-1])
    upper_turned = turned.transpose(1, 0, 2, 3).reshape(nb, nb)

    lt = lower_inv.T.reshape(2, 4, 2, share, nb)
    lt = jnp.where(half == 0, lt, lt[::-1])
    lt = lax.dynamic_slice_in_dim(jnp.concatenate([lt, lt], 1), x, 4, 1)
    lt = jnp.where(core == 0, lt, lt[:, :, ::-1])
    lower_turned = lt.transpose(2, 1, 0, 3, 4).reshape(nb, nb)
    b_all = jnp.concatenate([b_mine, b_theirs], 0)

    first = (((0,), (0,)), ((), ()))
    lower_full = lax.dot_general(
        a_all, upper_turned, first, preferred_element_type=jnp.float32
    ).astype(jnp.bfloat16)
    upper_full = lax.dot_general(
        lower_turned, b_all, first, preferred_element_type=jnp.float32
    ).astype(jnp.bfloat16)
    product = jnp.dot(lower_full, upper_full, preferred_element_type=jnp.float32)
    lower_tile = lax.dynamic_slice_in_dim(lower_full, col * share, share, 1)
    upper_tile = lax.dynamic_slice_in_dim(upper_full, row * share, share, 0)
    return lower_tile, upper_tile, trailing - product


def solution(mesh):
    in_specs = (P("row", "col"), P("row", "col"), P("row", "col"), P(), P())
    out_specs = (P("row", "col"), P("row", "col"), P("row", "col"))
    return jax.shard_map(
        on_device, mesh=mesh, in_specs=in_specs, out_specs=out_specs, check_vma=False
    )
```

time: 156 us -> 73.2 us (0.47)
  waiting for transfers between devices: 127 us -> 12.5 us
  starting transfers between devices: 0.08 us -> 24.6 us
  local copies, waits for them, and re-layouts: 2.73 us -> 20.2 us
  between operations: 14.1 us -> 0.84 us
  other arithmetic: 0 us -> 5.29 us
  matrix products: 11.4 us -> 9.44 us
    all_gather x2 -> x0, waiting for transfers between devices: 126 us -> none  [the longest x1 66 us: on_device(): lax.all_gather(column_block, 'col', axis=1, tiled=True)]
    ppermute x0 -> x14, starting transfers between devices: none -> 24.6 us  [send(): return lax.ppermute(block, ('row', 'col'), pairs_of(16, 16, target))]
    unnamed x9 -> x37, local copies, waits for them, and re-layouts: 1.93 us -> 15.9 us
    ppermute x0 -> x14, waiting for transfers between devices: none -> 12.5 us  [send(): return lax.ppermute(block, ('row', 'col'), pairs_of(16, 16, target))]
    concatenate x0 -> x4, other arithmetic: none -> 3.59 us  [the longest x1 2.78 us: on_device(): jnp.concatenate([upper_inv, upper_inv], 0)]
    dot_general x2, matrix products: 7.96 us -> 5.98 us  [the longest x1 4.13 us: on_device(): lax.dot_general(lower_turned, b_all, first, preferred_element_type=jnp.fl...]
    concatenate x0 -> x3, local copies, waits for them, and re-layouts: none -> 1.8 us  [the longest x1 1.03 us: on_device(): b_all = jnp.concatenate([b_mine, b_theirs], 0)]
    transpose x0 -> x2, local copies, waits for them, and re-layouts: none -> 1.66 us  [the longest x1 1.49 us: on_device(): lower_turned = lt.transpose(2, 1, 0, 3, 4).reshape(nb, nb)]
  transfers between devices with their start and end apart: 2 -> 14, of which waited for: 2 -> 3; matrix products, arithmetic and copies ran while one was open for 3% -> 31% of each run, Pallas kernels for 0% -> 0%
where the time goes in v1:
time: 73.2 us; the launch traced here: 72.9 us
  starting transfers between devices  24.6 us (34%)
  local copies, waits for them, and re-layouts  20.2 us (28%)
  waiting for transfers between devices  12.5 us (17%)
  matrix products  9.44 us (13%)
  other arithmetic  5.29 us (7%)
  between operations  0.84 us (1%)
    ppermute x14, starting transfers between devices, send(): return lax.ppermute(block, ('row', 'col'), pairs_of(16, 16, target))  24.6 us
    unnamed x37, local copies, waits for them, and re-layouts  15.9 us
    ppermute x14, waiting for transfers between devices, send(): return lax.ppermute(block, ('row', 'col'), pairs_of(16, 16, target))  12.5 us
    dot_general x1, matrix products, on_device(): lax.dot_general(lower_turned, b_all, first, preferred_element_type=jnp.fl...  4.13 us
    dot_general x1, matrix products, on_device(): jnp.dot(lower_full, upper_full, preferred_element_type=jnp.float32)  3.47 us
    concatenate x1, other arithmetic, on_device(): jnp.concatenate([upper_inv, upper_inv], 0)  2.78 us
    dot_general x1, matrix products, on_device(): lax.dot_general(a_all, upper_turned, first, preferred_element_type=jnp.fl...  1.85 us
    transpose x1, local copies, waits for them, and re-layouts, on_device(): lower_turned = lt.transpose(2, 1, 0, 3, 4).reshape(nb, nb)  1.49 us
  transfers between devices with their start and end apart: 14, of which 3 were waited for; matrix products, arithmetic and copies ran while one was open for 31% of the time, Pallas kernels for 0%

profile of v1, /device:TPU:1, one launch (start us, length us, event | category | flops | bytes accessed | tf_op | source)
XLA Modules:
  0.0 72.9 jit_solution(17855735317986927214)
XLA Ops:
  0.6 6.5 %collective-permute-start = (bf16[64,768]{1,0:T(8,128)(2,1)}, bf16[64,768]{1,0:T(8,128)(2,1)S(1)}, u32[]{:S(2)}, u32[]{:S(2)}) collective-permute-start(bf16[64,768]{1,0:T(8,128)(2,1)} %bitcast.22), channel_id=1, source_target_pairs={{0,14},{1,15},{2,0},{3,1},{4,2},{5,3},{6,4},{7,5},{8,6},{9,7},{10,... | collective-permute-start | bytes 294920 | tf_op jit(solution)/shard_map/ppermute | solution.py:24
  7.1 1.4 %collective-permute-start.1 = (bf16[64,768]{1,0:T(8,128)(2,1)}, bf16[64,768]{1,0:T(8,128)(2,1)S(1)}, u32[]{:S(2)}, u32[]{:S(2)}) collective-permute-start(bf16[64,768]{1,0:T(8,128)(2,1)} %bitcast.23), channel_id=1, source_target_pairs={{0,8},{1,9},{2,10},{3,11},{4,12},{5,13},{6,14},{7,15},{8,0},{9,1},... | collective-permute-start | bytes 294920 | tf_op jit(solution)/shard_map/ppermute | solution.py:24
  8.5 1.4 %collective-permute-start.3 = (bf16[64,768]{1,0:T(8,128)(2,1)}, bf16[64,768]{1,0:T(8,128)(2,1)S(1)}, u32[]{:S(2)}, u32[]{:S(2)}) collective-permute-start(bf16[64,768]{1,0:T(8,128)(2,1)} %bitcast.24), channel_id=1, source_target_pairs={{0,2},{1,3},{2,4},{3,5},{4,6},{5,7},{6,8},{7,9},{8,10},{9,11},{10,... | collective-permute-start | bytes 294920 | tf_op jit(solution)/shard_map/ppermute | solution.py:24
  9.9 1.3 %collective-permute-start.5 = (bf16[64,768]{1,0:T(8,128)(2,1)}, bf16[64,768]{1,0:T(8,128)(2,1)S(1)}, u32[]{:S(2)}, u32[]{:S(2)}) collective-permute-start(bf16[64,768]{1,0:T(8,128)(2,1)} %bitcast.25), channel_id=1, source_target_pairs={{0,1},{1,0},{2,3},{3,2},{4,5},{5,4},{6,7},{7,6},{8,9},{9,8},{10,11... | collective-permute-start | bytes 294920 | tf_op jit(solution)/shard_map/ppermute | solution.py:24
  11.2 2.6 %collective-permute-start.9 = (bf16[64,1024]{1,0:T(8,128)(2,1)}, bf16[64,1024]{1,0:T(8,128)(2,1)S(1)}, u32[]{:S(2)}, u32[]{:S(2)}) collective-permute-start(bf16[64,1024]{1,0:T(8,128)(2,1)} %param.7), channel_id=1, source_target_pairs={{0,128},{1,129},{2,130},{3,131},{4,132},{5,133},{6,134},{7,135},{8... | collective-permute-start | bytes 393224 | tf_op jit(solution)/shard_map/ppermute | solution.py:24
  13.8 1.5 %constant_dynamic-update-slice_fusion.4 = bf16[1024,768]{1,0:T(8,128)(2,1)} fusion(bf16[768,64]{0,1:T(8,128)(2,1)} %param.6), kind=kLoop, calls=%fused_computation.32 | loop fusion | bytes 196608
  15.4 2.9 %copy.13 = bf16[1024,1024]{0,1:T(8,128)(2,1)S(1)} copy(bf16[1024,1024]{1,0:T(8,128)(2,1)} %param.8) | data formatting | bytes 4194304 | tf_op args[3]
  20.2 1.5 %copy.14 = bf16[2,4,2,64,1024]{4,3,2,1,0:T(8,128)(2,1)} copy(bf16[2,4,2,64,1024]{4,3,0,1,2:T(8,128)(2,1)S(1)} %fusion.1) | data formatting | bytes 4194304 | tf_op jit(solution)/shard_map/transpose | solution.py:85
  21.7 0.8 %copy-done = bf16[1024,1024]{1,0:T(8,128)(2,1)S(1)} copy-done((bf16[1024,1024]{1,0:T(8,128)(2,1)S(1)}, bf16[1024,1024]{1,0:T(8,128)(2,1)}, u32[]{:S(2)}) %copy-start) | copy-done | bytes 2097176
  22.5 2.8 %fusion.3 = bf16[1024,1024]{1,0:T(8,128)(2,1)S(1)} fusion(s32[]{:T(128)S(6)} %select_n.35, bf16[1024,1024]{1,0:T(8,128)(2,1)S(1)} %copy-done), kind=kLoop, calls=%fused_computation.10 | loop fusion | flops 4194304 | bytes 4194308 | tf_op jit(solution)/shard_map/concatenate | solution.py:76
  27.5 1.4 %collective-permute-start.2 = (bf16[128,768]{1,0:T(8,128)(2,1)S(1)}, bf16[128,768]{1,0:T(8,128)(2,1)S(1)}, u32[]{:S(2)}, u32[]{:S(2)}) collective-permute-start(bf16[128,768]{1,0:T(8,128)(2,1)S(1)} %get-tuple-element.27), channel_id=1, source_target_pairs={{0,14},{1,15},{2,0},{3,1},{4,2},{5,3},{6,4},{7,5},{8,6},{9,7},{10,... | collective-permute-start | bytes 589832 | tf_op jit(solution)/shard_map/ppermute | solution.py:24
  30.5 2.5 %collective-permute-start.10 = (bf16[128,1024]{1,0:T(8,128)(2,1)S(1)}, bf16[128,1024]{1,0:T(8,128)(2,1)S(1)}, u32[]{:S(2)}, u32[]{:S(2)}) collective-permute-start(bf16[128,1024]{1,0:T(8,128)(2,1)S(1)} %get-tuple-element.22), channel_id=1, source_target_pairs={{0,96},{1,97},{2,98},{3,99},{4,100},{5,101},{6,102},{7,103},{8,104... | collective-permute-start | bytes 786440 | tf_op jit(solution)/shard_map/ppermute | solution.py:24
  33.0 1.9 %collective-permute-start.11 = (bf16[128,1024]{1,0:T(8,128)(2,1)S(1)}, bf16[128,1024]{1,0:T(8,128)(2,1)S(1)}, u32[]{:S(2)}, u32[]{:S(2)}) collective-permute-start(bf16[128,1024]{1,0:T(8,128)(2,1)S(1)} %get-tuple-element.22), channel_id=1, source_target_pairs={{0,64},{1,65},{2,66},{3,67},{4,68},{5,69},{6,70},{7,71},{8,72},{9,... | collective-permute-start | bytes 786440 | tf_op jit(solution)/shard_map/ppermute | solution.py:24
  41.2 5.1 %collective-permute-done.12 = bf16[128,1024]{1,0:T(8,128)(2,1)S(1)} collective-permute-done((bf16[128,1024]{1,0:T(8,128)(2,1)S(1)}, bf16[128,1024]{1,0:T(8,128)(2,1)S(1)}, u32[]{:S(2)}, u32[]{:S(2)}) %collective-permute-start.12) | collective-permute-done | bytes 262176 | tf_op jit(solution)/shard_map/ppermute | solution.py:24
  47.1 2.5 %collective-permute-start.13 = (bf16[512,1024]{1,0:T(8,128)(2,1)}, bf16[512,1024]{1,0:T(8,128)(2,1)S(1)}, u32[]{:S(2)}, u32[]{:S(2)}) collective-permute-start(bf16[512,1024]{1,0:T(8,128)(2,1)} %get-tuple-element.14), channel_id=1, source_target_pairs={{0,16},{1,17},{2,18},{3,19},{4,20},{5,21},{6,22},{7,23},{8,24},{9,... | collective-permute-start | bytes 3145736 | tf_op jit(solution)/shard_map/ppermute | solution.py:24
  49.6 2.6 %collective-permute-start.7 = (bf16[128,768]{1,0:T(8,128)(2,1)S(1)}, bf16[128,768]{1,0:T(8,128)(2,1)S(1)}, u32[]{:S(2)}, u32[]{:S(2)}) collective-permute-start(bf16[128,768]{1,0:T(8,128)(2,1)S(1)} %get-tuple-element.13), channel_id=1, source_target_pairs={{0,14},{1,15},{2,0},{3,1},{4,2},{5,3},{6,4},{7,5},{8,6},{9,7},{10,... | collective-permute-start | bytes 589832 | tf_op jit(solution)/shard_map/ppermute | solution.py:24
  52.2 4.3 %collective-permute-done.7 = bf16[128,768]{1,0:T(8,128)(2,1)S(1)} collective-permute-done((bf16[128,768]{1,0:T(8,128)(2,1)S(1)}, bf16[128,768]{1,0:T(8,128)(2,1)S(1)}, u32[]{:S(2)}, u32[]{:S(2)}) %collective-permute-start.7) | collective-permute-done | bytes 196640 | tf_op jit(solution)/shard_map/ppermute | solution.py:24
  56.5 3.1 %collective-permute-done.8 = bf16[128,768]{1,0:T(8,128)(2,1)S(1)} collective-permute-done((bf16[128,768]{1,0:T(8,128)(2,1)S(1)}, bf16[128,768]{1,0:T(8,128)(2,1)S(1)}, u32[]{:S(2)}, u32[]{:S(2)}) %collective-permute-start.8) | collective-permute-done | bytes 196640 | tf_op jit(solution)/shard_map/ppermute | solution.py:24
  59.7 1.8 %convolution_convert_fusion.1 = bf16[768,1024]{1,0:T(8,128)(2,1)S(1)} fusion(bf16[1024,768]{1,0:T(8,128)(2,1)S(1)} %slice_dynamic-update-slice_fusion, bf16[1024,1024]{1,0:T(8,128)(2,1)S(1)} %bitcast.21), kind=kOutput, calls=%fused_computation.13 | convolution fusion | flops 1611399168 | bytes 5242880 | tf_op jit(solution)/shard_map/dot_general | solution.py:89
  61.6 1.1 %copy-done.3 = bf16[768,1024]{1,0:T(8,128)(2,1)} copy-done((bf16[768,1024]{1,0:T(8,128)(2,1)}, bf16[768,1024]{1,0:T(8,128)(2,1)S(1)}, u32[]{:S(2)}) %copy-start.3) | copy-done | bytes 1572888
  62.8 0.8 %copy.15 = bf16[768,64]{0,1:T(8,128)(2,1)} copy(bf16[768,64]{1,0:T(8,128)(2,1)S(1)} %constant_dynamic-slice_fusion.1) | data formatting | bytes 196608
  63.6 1.0 %constant_dynamic-update-slice_fusion.12 = bf16[1024,1024]{1,0:T(8,128)(2,1)} fusion(bf16[1024,1024]{1,0:T(8,128)(2,1)} %copy-done.5, bf16[512,1024]{1,0:T(8,128)(2,1)S(1)} %collective-permute-done.13), kind=kLoop, calls=%fused_computation.40 | loop fusion | bytes 2097152 | tf_op jit(solution)/shard_map/concatenate | solution.py:86
  64.7 4.1 %convolution_convert_fusion = bf16[1024,1024]{1,0:T(8,128)(2,1)S(1)} fusion(bf16[1024,1024]{1,0:T(8,128)(2,1)S(1)} %bitcast.20, bf16[1024,1024]{1,0:T(8,128)(2,1)} %constant_dynamic-update-slice_fusion.12), kind=kOutput, calls=%fused_computation.11 | convolution fusion | flops 2148532224 | bytes 6291456 | tf_op jit(solution)/shard_map/dot_general | solution.py:92
  68.8 3.5 %convolution_subtract_fusion = f32[768,1024]{1,0:T(8,128)} fusion(f32[768,1024]{1,0:T(8,128)S(1)} %copy-done.7, bf16[768,1024]{1,0:T(8,128)(2,1)S(1)} %copy-done.4, bf16[1024,1024]{1,0:T(8,128)(2,1)S(1)} %convolution_convert_fusion), kind=kOutput, calls=%fused_computation.12 | convolution fusion | flops 1611399168 | bytes 9961472 | tf_op jit(solution)/shard_map/dot_general | solution.py:95
  (59 shorter events, 13.7 us)
Async XLA Ops:
  0.6 26.8 %collective-permute-start = (bf16[64,768]{1,0:T(8,128)(2,1)}, bf16[64,768]{1,0:T(8,128)(2,1)S(1)}, u32[]{:S(2)}, u32[]{:S(2)}) collective-permute-start(bf16[64,768]{1,0:T(8,128)(2,1)} %bitcast.22), channel_id=1, source_target_pairs={{0,14},{1,15},{2,0},{3,1},{4,2},{5,3},{6,4},{7,5},{8,6},{9,7},{10,... | collective-permute-start | bytes 294920 | tf_op jit(solution)/shard_map/ppermute | solution.py:24
  7.1 20.3 %collective-permute-start.1 = (bf16[64,768]{1,0:T(8,128)(2,1)}, bf16[64,768]{1,0:T(8,128)(2,1)S(1)}, u32[]{:S(2)}, u32[]{:S(2)}) collective-permute-start(bf16[64,768]{1,0:T(8,128)(2,1)} %bitcast.23), channel_id=1, source_target_pairs={{0,8},{1,9},{2,10},{3,11},{4,12},{5,13},{6,14},{7,15},{8,0},{9,1},... | collective-permute-start | bytes 294920 | tf_op jit(solution)/shard_map/ppermute | solution.py:24
  8.5 18.9 %collective-permute-start.3 = (bf16[64,768]{1,0:T(8,128)(2,1)}, bf16[64,768]{1,0:T(8,128)(2,1)S(1)}, u32[]{:S(2)}, u32[]{:S(2)}) collective-permute-start(bf16[64,768]{1,0:T(8,128)(2,1)} %bitcast.24), channel_id=1, source_target_pairs={{0,2},{1,3},{2,4},{3,5},{4,6},{5,7},{6,8},{7,9},{8,10},{9,11},{10,... | collective-permute-start | bytes 294920 | tf_op jit(solution)/shard_map/ppermute | solution.py:24
  9.9 29.1 %collective-permute-start.5 = (bf16[64,768]{1,0:T(8,128)(2,1)}, bf16[64,768]{1,0:T(8,128)(2,1)S(1)}, u32[]{:S(2)}, u32[]{:S(2)}) collective-permute-start(bf16[64,768]{1,0:T(8,128)(2,1)} %bitcast.25), channel_id=1, source_target_pairs={{0,1},{1,0},{2,3},{3,2},{4,5},{5,4},{6,7},{7,6},{8,9},{9,8},{10,11... | collective-permute-start | bytes 294920 | tf_op jit(solution)/shard_map/ppermute | solution.py:24
  11.2 18.6 %collective-permute-start.9 = (bf16[64,1024]{1,0:T(8,128)(2,1)}, bf16[64,1024]{1,0:T(8,128)(2,1)S(1)}, u32[]{:S(2)}, u32[]{:S(2)}) collective-permute-start(bf16[64,1024]{1,0:T(8,128)(2,1)} %param.7), channel_id=1, source_target_pairs={{0,128},{1,129},{2,130},{3,131},{4,132},{5,133},{6,134},{7,135},{8... | collective-permute-start | bytes 393224 | tf_op jit(solution)/shard_map/ppermute | solution.py:24
  20.2 2.4 %copy-start = (bf16[1024,1024]{1,0:T(8,128)(2,1)S(1)}, bf16[1024,1024]{1,0:T(8,128)(2,1)}, u32[]{:S(2)}) copy-start(bf16[1024,1024]{1,0:T(8,128)(2,1)} %param.9) | copy-start | bytes 6291460
  25.9 0.9 %copy-start.2 = (bf16[64,1024]{1,0:T(8,128)(2,1)S(1)}, bf16[64,1024]{1,0:T(8,128)(2,1)}, u32[]{:S(2)}) copy-start(bf16[64,1024]{1,0:T(8,128)(2,1)} %param.7) | copy-start | bytes 393220
  27.5 5.5 %collective-permute-start.2 = (bf16[128,768]{1,0:T(8,128)(2,1)S(1)}, bf16[128,768]{1,0:T(8,128)(2,1)S(1)}, u32[]{:S(2)}, u32[]{:S(2)}) collective-permute-start(bf16[128,768]{1,0:T(8,128)(2,1)S(1)} %get-tuple-element.27), channel_id=1, source_target_pairs={{0,14},{1,15},{2,0},{3,1},{4,2},{5,3},{6,4},{7,5},{8,6},{9,7},{10,... | collective-permute-start | bytes 589832 | tf_op jit(solution)/shard_map/ppermute | solution.py:24
  28.9 6.6 %collective-permute-start.4 = (bf16[128,768]{1,0:T(8,128)(2,1)S(1)}, bf16[128,768]{1,0:T(8,128)(2,1)S(1)}, u32[]{:S(2)}, u32[]{:S(2)}) collective-permute-start(bf16[128,768]{1,0:T(8,128)(2,1)S(1)} %get-tuple-element.26), channel_id=1, source_target_pairs={{0,2},{1,3},{2,4},{3,5},{4,6},{5,7},{6,8},{7,9},{8,10},{9,11},{10,... | collective-permute-start | bytes 589832 | tf_op jit(solution)/shard_map/ppermute | solution.py:24
  29.1 20.5 %collective-permute-start.6 = (bf16[192,768]{1,0:T(8,128)(2,1)S(1)}, bf16[192,768]{1,0:T(8,128)(2,1)S(1)}, u32[]{:S(2)}, u32[]{:S(2)}) collective-permute-start(bf16[192,768]{1,0:T(8,128)(2,1)S(1)} %pad_maximum_fusion), channel_id=1, source_target_pairs={{0,1},{1,0},{2,3},{3,2},{4,5},{5,4},{6,7},{7,6},{8,9},{9,8},{10,11... | collective-permute-start | bytes 884744 | tf_op jit(solution)/shard_map/ppermute | solution.py:24
  30.5 9.2 %collective-permute-start.10 = (bf16[128,1024]{1,0:T(8,128)(2,1)S(1)}, bf16[128,1024]{1,0:T(8,128)(2,1)S(1)}, u32[]{:S(2)}, u32[]{:S(2)}) collective-permute-start(bf16[128,1024]{1,0:T(8,128)(2,1)S(1)} %get-tuple-element.22), channel_id=1, source_target_pairs={{0,96},{1,97},{2,98},{3,99},{4,100},{5,101},{6,102},{7,103},{8,104... | collective-permute-start | bytes 786440 | tf_op jit(solution)/shard_map/ppermute | solution.py:24
  33.0 7.5 %collective-permute-start.11 = (bf16[128,1024]{1,0:T(8,128)(2,1)S(1)}, bf16[128,1024]{1,0:T(8,128)(2,1)S(1)}, u32[]{:S(2)}, u32[]{:S(2)}) collective-permute-start(bf16[128,1024]{1,0:T(8,128)(2,1)S(1)} %get-tuple-element.22), channel_id=1, source_target_pairs={{0,64},{1,65},{2,66},{3,67},{4,68},{5,69},{6,70},{7,71},{8,72},{9,... | collective-permute-start | bytes 786440 | tf_op jit(solution)/shard_map/ppermute | solution.py:24
  35.5 10.8 %collective-permute-start.12 = (bf16[128,1024]{1,0:T(8,128)(2,1)S(1)}, bf16[128,1024]{1,0:T(8,128)(2,1)S(1)}, u32[]{:S(2)}, u32[]{:S(2)}) collective-permute-start(bf16[128,1024]{1,0:T(8,128)(2,1)S(1)} %get-tuple-element.22), channel_id=1, source_target_pairs={{0,32},{1,33},{2,34},{3,35},{4,36},{5,37},{6,38},{7,39},{8,40},{9,... | collective-permute-start | bytes 786440 | tf_op jit(solution)/shard_map/ppermute | solution.py:24
  39.7 12.5 %copy-start.6 = (bf16[1024,768]{1,0:T(8,128)(2,1)S(1)}, bf16[1024,768]{1,0:T(8,128)(2,1)}, u32[]{:S(2)}) copy-start(bf16[1024,768]{1,0:T(8,128)(2,1)} %constant_dynamic-update-slice_fusion) | copy-start | bytes 4718596
  47.1 12.7 %copy-start.5 = (bf16[1024,1024]{1,0:T(8,128)(2,1)}, bf16[1024,1024]{1,0:T(8,128)(2,1)S(1)}, u32[]{:S(2)}) copy-start(bf16[1024,1024]{1,0:T(8,128)(2,1)S(1)} %get-tuple-element.15) | copy-start | bytes 6291460
  47.1 16.6 %collective-permute-start.13 = (bf16[512,1024]{1,0:T(8,128)(2,1)}, bf16[512,1024]{1,0:T(8,128)(2,1)S(1)}, u32[]{:S(2)}, u32[]{:S(2)}) collective-permute-start(bf16[512,1024]{1,0:T(8,128)(2,1)} %get-tuple-element.14), channel_id=1, source_target_pairs={{0,16},{1,17},{2,18},{3,19},{4,20},{5,21},{6,22},{7,23},{8,24},{9,... | collective-permute-start | bytes 3145736 | tf_op jit(solution)/shard_map/ppermute | solution.py:24
  49.6 6.9 %collective-permute-start.7 = (bf16[128,768]{1,0:T(8,128)(2,1)S(1)}, bf16[128,768]{1,0:T(8,128)(2,1)S(1)}, u32[]{:S(2)}, u32[]{:S(2)}) collective-permute-start(bf16[128,768]{1,0:T(8,128)(2,1)S(1)} %get-tuple-element.13), channel_id=1, source_target_pairs={{0,14},{1,15},{2,0},{3,1},{4,2},{5,3},{6,4},{7,5},{8,6},{9,7},{10,... | collective-permute-start | bytes 589832 | tf_op jit(solution)/shard_map/ppermute | solution.py:24
  52.2 7.4 %collective-permute-start.8 = (bf16[128,768]{1,0:T(8,128)(2,1)S(1)}, bf16[128,768]{1,0:T(8,128)(2,1)S(1)}, u32[]{:S(2)}, u32[]{:S(2)}) collective-permute-start(bf16[128,768]{1,0:T(8,128)(2,1)S(1)} %get-tuple-element.12), channel_id=1, source_target_pairs={{0,2},{1,3},{2,4},{3,5},{4,6},{5,7},{6,8},{7,9},{8,10},{9,11},{10,... | collective-permute-start | bytes 589832 | tf_op jit(solution)/shard_map/ppermute | solution.py:24
  61.6 1.1 %copy-start.3 = (bf16[768,1024]{1,0:T(8,128)(2,1)}, bf16[768,1024]{1,0:T(8,128)(2,1)S(1)}, u32[]{:S(2)}) copy-start(bf16[768,1024]{1,0:T(8,128)(2,1)S(1)} %convolution_convert_fusion.1) | copy-start | bytes 4718596
  62.7 1.9 %copy-start.1 = (bf16[2,4,2,64,1024]{4,3,2,1,0:T(8,128)(2,1)S(1)}, bf16[2,4,2,64,1024]{4,3,2,1,0:T(8,128)(2,1)}, u32[]{:S(2)}) copy-start(bf16[2,4,2,64,1024]{4,3,2,1,0:T(8,128)(2,1)} %copy.14) | copy-start | bytes 6291460
  64.6 4.1 %copy-start.4 = (bf16[768,1024]{1,0:T(8,128)(2,1)S(1)}, bf16[768,1024]{1,0:T(8,128)(2,1)}, u32[]{:S(2)}) copy-start(bf16[768,1024]{1,0:T(8,128)(2,1)} %copy-done.3) | copy-start | bytes 4718596
  64.7 4.1 %copy-start.7 = (f32[768,1024]{1,0:T(8,128)S(1)}, f32[768,1024]{1,0:T(8,128)}, u32[]{:S(2)}) copy-start(f32[768,1024]{1,0:T(8,128)} %param.5) | copy-start | bytes 9437188

commit v2 on v1

v2 whole, which is shorter than its diff:
```python
import functools

import jax
import jax.numpy as jnp
from jax import lax
from jax.experimental import pallas as pl
from jax.experimental.pallas import tpu as pltpu
from jax.sharding import PartitionSpec as P

VMEM = pl.BlockSpec(memory_space=pltpu.VMEM)
HBM = pl.BlockSpec(memory_space=pltpu.HBM)
FIRST = (((0,), (0,)), ((), ()))
BLOCK = 256


def split(row, col):
    return row >> 3, (row >> 1) & 3, row & 1, col >> 1, col & 1


def pairs_of(rows, cols, target):
    pairs = []
    for row in range(rows):
        for col in range(cols):
            half, x, core, z, low = target(*split(row, col))
            to_row = ((half % 2) * 4 + x % 4) * 2 + core
            to_col = (z % 8) * 2 + low
            pairs.append((row * cols + col, to_row * cols + to_col))
    return pairs


def place():
    return split(lax.axis_index("row"), lax.axis_index("col"))


def put(full_ref, at, piece_ref, index, share):
    rows = pl.ds(pl.multiple_of(at * share, share), share)
    full_ref[rows, :] = piece_ref[index * share : (index + 1) * share, :]


def upper_kernel(places, *refs):
    *piece_refs, lower_ref, full_ref, tile_ref, b_ref, sem = refs
    half, x, core, _, _ = place()
    share = tile_ref.shape[0]
    for ref, shards in zip(piece_refs, places, strict=True):
        for index, (dx, dhalf, dcore) in enumerate(shards):
            at = ((half ^ dhalf) * 4 + lax.rem(x + dx, 4)) * 2 + (core ^ dcore)
            put(b_ref, at, ref, index, share)
    for i in range(full_ref.shape[0] // BLOCK):
        rows, known = slice(i * BLOCK, (i + 1) * BLOCK), (i + 1) * BLOCK
        full_ref[rows, :] = jnp.dot(
            lower_ref[rows, :known], b_ref[:known, :], preferred_element_type=jnp.float32
        ).astype(full_ref.dtype)
    own = pl.ds(pl.multiple_of(lax.axis_index("row") * share, share), share)
    copy = pltpu.make_async_copy(full_ref.at[own, :], tile_ref, sem)
    copy.start()
    copy.wait()


def update_kernel(places, *refs):
    *piece_refs, upper_inv_ref, upper_ref, trailing_ref = refs[: len(places) + 3]
    tile_ref, updated_ref, a_ref, lower_ref, out_ref, tile_sem, out_sems = refs[len(places) + 3 :]
    _, _, _, z, low = place()
    share = tile_ref.shape[0]
    for ref, shards in zip(piece_refs, places, strict=True):
        for index, (dz, dlow) in enumerate(shards):
            put(a_ref, lax.rem(z + dz, 8) * 2 + (low ^ dlow), ref, index, share)
    blocks = upper_ref.shape[1] // BLOCK
    for j in range(blocks):
        cols, known = slice(j * BLOCK, (j + 1) * BLOCK), (j + 1) * BLOCK
        lower_ref[cols, :] = lax.dot_general(
            upper_inv_ref[:known, cols], a_ref[:known, :], FIRST, preferred_element_type=jnp.float32
        ).astype(lower_ref.dtype)
    own = pl.ds(pl.multiple_of(lax.axis_index("col") * share, share), share)
    tile_copy = pltpu.make_async_copy(lower_ref.at[own, :], tile_ref, tile_sem)
    tile_copy.start()
    copies = []
    for j in range(blocks):
        cols = slice(j * BLOCK, (j + 1) * BLOCK)
        out_ref[:, cols] = trailing_ref[:, cols] - lax.dot_general(
            lower_ref[...], upper_ref[:, cols], FIRST, preferred_element_type=jnp.float32
        )
        copies.append(
            pltpu.make_async_copy(out_ref.at[:, cols], updated_ref.at[:, cols], out_sems.at[j])
        )
        copies[-1].start()
    tile_copy.wait()
    for copy in copies:
        copy.wait()


def on_device(trailing, column_block, row_block, lower_inv, upper_inv):
    def send(block, target):
        return lax.ppermute(block, ("row", "col"), pairs_of(16, 16, target))

    def from_z(block, step):
        return send(block, lambda half, x, core, z, low: (half, x, core, z - step, low))

    def from_x(block, step):
        return send(block, lambda half, x, core, z, low: (half, x - step, core, z, low))

    def from_half(block):
        return send(block, lambda half, x, core, z, low: (half ^ 1, x, core, z, low))

    def from_low(block):
        return send(block, lambda half, x, core, z, low: (half, x, core, z, low ^ 1))

    def from_core(block):
        return send(block, lambda half, x, core, z, low: (half, x, core ^ 1, z, low))

    rows, cols = trailing.shape
    nb = upper_inv.shape[0]
    share = column_block.shape[1]
    own_a, own_b = column_block.T, row_block

    a_next, a_prev = from_z(own_a, 1), from_z(own_a, -1)
    other_half = from_half(own_b)
    a_far = from_z(own_a, 4)
    other_low = from_low(own_a)

    b_x = [jnp.concatenate([own_b, other_half], 0)]
    b_x += [from_x(b_x[0], step) for step in (1, 3, 2)]
    b_core = [from_core(block) for block in b_x]

    three = jnp.concatenate([a_next, a_far, a_prev], 0)
    up = from_z(three[: 2 * share], 1)
    down = from_z(three[share:], -1)
    low_three = from_low(three)
    low_up = from_z(low_three[: 2 * share], 1)
    low_down = from_z(low_three[share:], -1)

    steps = (0, 1, 3, 2)
    b_places = [[(dx, dhalf, dcore) for dhalf in (0, 1)] for dcore in (0, 1) for dx in steps]
    upper_full, upper_tile = pl.pallas_call(
        functools.partial(upper_kernel, b_places),
        out_shape=[
            jax.ShapeDtypeStruct((nb, cols), jnp.bfloat16),
            jax.ShapeDtypeStruct(row_block.shape, jnp.bfloat16),
        ],
        in_specs=[VMEM] * 9,
        out_specs=[VMEM, HBM],
        scratch_shapes=[pltpu.VMEM((nb, cols), jnp.bfloat16), pltpu.SemaphoreType.DMA],
        compiler_params=pltpu.CompilerParams(vmem_limit_bytes=8 << 20),
        cost_estimate=pl.CostEstimate(flops=2 * nb * nb * cols, bytes_accessed=0, transcendentals=0),
    )(*b_x, *b_core, lower_inv)

    a_places = [
        [(0, 0)], [(1, 0), (4, 0), (7, 0)], [(2, 0), (5, 0)], [(3, 0), (6, 0)],
        [(0, 1)], [(1, 1), (4, 1), (7, 1)], [(2, 1), (5, 1)], [(3, 1), (6, 1)],
    ]
    lower_tile, updated = pl.pallas_call(
        functools.partial(update_kernel, a_places),
        out_shape=[
            jax.ShapeDtypeStruct((share, rows), jnp.bfloat16),
            jax.ShapeDtypeStruct((rows, cols), jnp.float32),
        ],
        in_specs=[VMEM] * (len(a_places) + 3),
        out_specs=[HBM, HBM],
        scratch_shapes=[
            pltpu.VMEM((nb, rows), jnp.bfloat16),
            pltpu.VMEM((nb, rows), jnp.bfloat16),
            pltpu.VMEM((rows, cols), jnp.float32),
            pltpu.SemaphoreType.DMA,
            pltpu.SemaphoreType.DMA((cols // BLOCK,)),
        ],
        compiler_params=pltpu.CompilerParams(vmem_limit_bytes=12 << 20),
        cost_estimate=pl.CostEstimate(flops=2 * rows * nb * (nb + cols), bytes_accessed=0, transcendentals=0),
    )(own_a, three, up, down, other_low, low_three, low_up, low_down, upper_inv, upper_full, trailing)
    return lower_tile.T, upper_tile, updated


def solution(mesh):
    in_specs = (P("row", "col"), P("row", "col"), P("row", "col"), P(), P())
    out_specs = (P("row", "col"), P("row", "col"), P("row", "col"))
    return jax.shard_map(
        on_device, mesh=mesh, in_specs=in_specs, out_specs=out_specs, check_vma=False
    )
```

time: 73.2 us -> 50.6 us (0.69)
  local copies, waits for them, and re-layouts: 20.2 us -> 1.03 us
  starting transfers between devices: 24.6 us -> 36.3 us
  matrix products: 9.44 us -> 0 us
  waiting for transfers between devices: 12.5 us -> 5.63 us
  Pallas kernels: 0 us -> 6.61 us
  other arithmetic: 5.29 us -> 0.03 us
    unnamed x37 -> x11, local copies, waits for them, and re-layouts: 15.9 us -> 0.99 us
    ppermute x14 -> x17, starting transfers between devices: 24.6 us -> 36.3 us  [send(): return lax.ppermute(block, ('row', 'col'), pairs_of(16, 16, target))]
    dot_general x3 -> x0, matrix products: 9.44 us -> none  [the longest x1 4.13 us: on_device(): lax.dot_general(lower_turned, b_all, first, preferred_element_type=jnp.fl...]
    ppermute x14 -> x17, waiting for transfers between devices: 12.5 us -> 5.63 us  [send(): return lax.ppermute(block, ('row', 'col'), pairs_of(16, 16, target))]
    pallas_call x0 -> x2, Pallas kernels: none -> 6.61 us  [the longest x1 4.27 us: on_device(): pl.pallas_call(functools.partial(update_kernel, a_places), out_shape=[jax...]
    concatenate x2 -> x0, other arithmetic: 3.54 us -> none  [the longest x1 2.78 us: on_device(): jnp.concatenate([upper_inv, upper_inv], 0)]
    concatenate x3 -> x2, local copies, waits for them, and re-layouts: 1.8 us -> 0.02 us  [the longest x1 0.01 us: on_device(): b_x = [jnp.concatenate([own_b, other_half], 0)]]
    transpose x2 -> x0, local copies, waits for them, and re-layouts: 1.66 us -> none  [the longest x1 1.49 us: on_device(): lower_turned = lt.transpose(2, 1, 0, 3, 4).reshape(nb, nb)]
  transfers between devices with their start and end apart: 14 -> 17, of which waited for: 3 -> 4; matrix products, arithmetic and copies ran while one was open for 31% -> 2% of each run, Pallas kernels for 0% -> 5%
where the time goes in v2:
time: 50.6 us; the launch traced here: 50.5 us
  starting transfers between devices  36.3 us (72%)
  Pallas kernels  6.61 us (13%)
  waiting for transfers between devices  5.63 us (11%)
  local copies, waits for them, and re-layouts  1.03 us (2%)
  between operations  0.94 us (2%)
    ppermute x17, starting transfers between devices, send(): return lax.ppermute(block, ('row', 'col'), pairs_of(16, 16, target))  36.3 us
    ppermute x17, waiting for transfers between devices, send(): return lax.ppermute(block, ('row', 'col'), pairs_of(16, 16, target))  5.63 us
    pallas_call x1, Pallas kernels, on_device(): pl.pallas_call(functools.partial(update_kernel, a_places), out_shape=[jax...  4.27 us
    pallas_call x1, Pallas kernels, on_device(): pl.pallas_call(functools.partial(upper_kernel, b_places), out_shape=[jax....  2.34 us
  transfers between devices with their start and end apart: 17, of which 4 were waited for; matrix products, arithmetic and copies ran while one was open for 2% of the time, Pallas kernels for 5%

profile of v2, /device:TPU:1, one launch (start us, length us, event | category | flops | bytes accessed | tf_op | source)
XLA Modules:
  0.0 50.5 jit_solution(10520205119365128349)
XLA Ops:
  0.6 2.5 %collective-permute-start.2 = (bf16[64,768]{1,0:T(8,128)(2,1)}, bf16[64,768]{1,0:T(8,128)(2,1)S(1)}, u32[]{:S(2)}, u32[]{:S(2)}) collective-permute-start(bf16[64,768]{1,0:T(8,128)(2,1)} %bitcast.2), channel_id=1, source_target_pairs={{0,2},{1,3},{2,4},{3,5},{4,6},{5,7},{6,8},{7,9},{8,10},{9,11},{10,... | collective-permute-start | bytes 294920 | tf_op jit(solution)/shard_map/ppermute | solution.py:93
  3.2 6.0 %collective-permute-start.1 = (bf16[64,768]{1,0:T(8,128)(2,1)}, bf16[64,768]{1,0:T(8,128)(2,1)S(1)}, u32[]{:S(2)}, u32[]{:S(2)}) collective-permute-start(bf16[64,768]{1,0:T(8,128)(2,1)} %bitcast.3), channel_id=1, source_target_pairs={{0,8},{1,9},{2,10},{3,11},{4,12},{5,13},{6,14},{7,15},{8,0},{9,1},... | collective-permute-start | bytes 294920 | tf_op jit(solution)/shard_map/ppermute | solution.py:93
  9.2 1.9 %collective-permute-start = (bf16[64,768]{1,0:T(8,128)(2,1)}, bf16[64,768]{1,0:T(8,128)(2,1)S(1)}, u32[]{:S(2)}, u32[]{:S(2)}) collective-permute-start(bf16[64,768]{1,0:T(8,128)(2,1)} %bitcast.4), channel_id=1, source_target_pairs={{0,14},{1,15},{2,0},{3,1},{4,2},{5,3},{6,4},{7,5},{8,6},{9,7},{10,... | collective-permute-start | bytes 294920 | tf_op jit(solution)/shard_map/ppermute | solution.py:93
  11.1 2.9 %collective-permute-start.9 = (bf16[64,1024]{1,0:T(8,128)(2,1)}, bf16[64,1024]{1,0:T(8,128)(2,1)S(1)}, u32[]{:S(2)}, u32[]{:S(2)}) collective-permute-start(bf16[64,1024]{1,0:T(8,128)(2,1)} %param.7), channel_id=1, source_target_pairs={{0,128},{1,129},{2,130},{3,131},{4,132},{5,133},{6,134},{7,135},{8... | collective-permute-start | bytes 393224 | tf_op jit(solution)/shard_map/ppermute | solution.py:93
  14.0 0.9 %constant_dynamic-update-slice_fusion.4 = bf16[128,1024]{1,0:T(8,128)(2,1)S(1)} fusion(bf16[64,1024]{1,0:T(8,128)(2,1)} %param.7), kind=kLoop, calls=%fused_computation.6 | loop fusion | bytes 262144
  15.0 1.2 %collective-permute-done = bf16[64,768]{1,0:T(8,128)(2,1)S(1)} collective-permute-done((bf16[64,768]{1,0:T(8,128)(2,1)}, bf16[64,768]{1,0:T(8,128)(2,1)S(1)}, u32[]{:S(2)}, u32[]{:S(2)}) %collective-permute-start) | collective-permute-done | bytes 98336 | tf_op jit(solution)/shard_map/ppermute | solution.py:93
  16.3 0.4 collective-permute-done.9
  16.7 2.8 %collective-permute-start.12 = (bf16[128,1024]{1,0:T(8,128)(2,1)S(1)}, bf16[128,1024]{1,0:T(8,128)(2,1)S(1)}, u32[]{:S(2)}, u32[]{:S(2)}) collective-permute-start(bf16[128,1024]{1,0:T(8,128)(2,1)S(1)} %constant_dynamic-update-slice_fusion.3.refs_0_), channel_id=1, source_target_pairs={{0,64},{1,65},{2,66},{3,67},{4,68},{5,69},{6,70},{7,71},{8,72},{9,... | collective-permute-start | bytes 786440 | tf_op jit(solution)/shard_map/ppermute | solution.py:93
  19.5 0.3 collective-permute-start.11
  19.8 2.4 %collective-permute-start.10 = (bf16[128,1024]{1,0:T(8,128)(2,1)S(1)}, bf16[128,1024]{1,0:T(8,128)(2,1)S(1)}, u32[]{:S(2)}, u32[]{:S(2)}) collective-permute-start(bf16[128,1024]{1,0:T(8,128)(2,1)S(1)} %constant_dynamic-update-slice_fusion.3.refs_0_), channel_id=1, source_target_pairs={{0,96},{1,97},{2,98},{3,99},{4,100},{5,101},{6,102},{7,103},{8,104... | collective-permute-start | bytes 786440 | tf_op jit(solution)/shard_map/ppermute | solution.py:93
  22.2 1.4 %collective-permute-start.6 = (bf16[192,768]{1,0:T(8,128)(2,1)S(1)}, bf16[192,768]{1,0:T(8,128)(2,1)S(1)}, u32[]{:S(2)}, u32[]{:S(2)}) collective-permute-start(bf16[192,768]{1,0:T(8,128)(2,1)S(1)} %constant_dynamic-update-slice_fusion.refs_1_), channel_id=1, source_target_pairs={{0,1},{1,0},{2,3},{3,2},{4,5},{5,4},{6,7},{7,6},{8,9},{9,8},{10,11... | collective-permute-start | bytes 884744 | tf_op jit(solution)/shard_map/ppermute | solution.py:93
  23.6 3.8 %collective-permute-start.13 = (bf16[128,1024]{1,0:T(8,128)(2,1)S(1)}, bf16[128,1024]{1,0:T(8,128)(2,1)S(1)}, u32[]{:S(2)}, u32[]{:S(2)}) collective-permute-start(bf16[128,1024]{1,0:T(8,128)(2,1)S(1)} %constant_dynamic-update-slice_fusion.3.refs_0_), channel_id=1, source_target_pairs={{0,16},{1,17},{2,18},{3,19},{4,20},{5,21},{6,22},{7,23},{8,24},{9,... | collective-permute-start | bytes 786440 | tf_op jit(solution)/shard_map/ppermute | solution.py:93
  27.4 2.5 %collective-permute-start.16 = (bf16[128,1024]{1,0:T(8,128)(2,1)S(1)}, bf16[128,1024]{1,0:T(8,128)(2,1)S(1)}, u32[]{:S(2)}, u32[]{:S(2)}) collective-permute-start(bf16[128,1024]{1,0:T(8,128)(2,1)S(1)} %collective-permute-done.12.refs_3_), channel_id=1, source_target_pairs={{0,16},{1,17},{2,18},{3,19},{4,20},{5,21},{6,22},{7,23},{8,24},{9,... | collective-permute-start | bytes 786440 | tf_op jit(solution)/shard_map/ppermute | solution.py:93
  29.8 0.6 %collective-permute-done.11.refs_2_ = bf16[128,1024]{1,0:T(8,128)(2,1)S(1)} collective-permute-done((bf16[128,1024]{1,0:T(8,128)(2,1)S(1)}, bf16[128,1024]{1,0:T(8,128)(2,1)S(1)}, u32[]{:S(2)}, u32[]{:S(2)}) %collective-permute-start.11) | collective-permute-done | bytes 262176 | tf_op jit(solution)/shard_map/ppermute | solution.py:93
  30.4 2.2 %collective-permute-start.15 = (bf16[128,1024]{1,0:T(8,128)(2,1)S(1)}, bf16[128,1024]{1,0:T(8,128)(2,1)S(1)}, u32[]{:S(2)}, u32[]{:S(2)}) collective-permute-start(bf16[128,1024]{1,0:T(8,128)(2,1)S(1)} %collective-permute-done.11.refs_2_), channel_id=1, source_target_pairs={{0,16},{1,17},{2,18},{3,19},{4,20},{5,21},{6,22},{7,23},{8,24},{9,... | collective-permute-start | bytes 786440 | tf_op jit(solution)/shard_map/ppermute | solution.py:93
  32.6 0.1 collective-permute-start.14
  32.7 1.4 %collective-permute-start.5 = (bf16[64,768]{1,0:T(8,128)(2,1)}, bf16[64,768]{1,0:T(8,128)(2,1)S(1)}, u32[]{:S(2)}, u32[]{:S(2)}) collective-permute-start(bf16[64,768]{1,0:T(8,128)(2,1)} %bitcast.5), channel_id=1, source_target_pairs={{0,1},{1,0},{2,3},{3,2},{4,5},{5,4},{6,7},{7,6},{8,9},{9,8},{10,11... | collective-permute-start | bytes 294920 | tf_op jit(solution)/shard_map/ppermute | solution.py:93
  34.2 1.3 %collective-permute-start.4 = (bf16[128,768]{1,0:T(8,128)(2,1)S(1)}, bf16[128,768]{1,0:T(8,128)(2,1)S(1)}, u32[]{:S(2)}, u32[]{:S(2)}) collective-permute-start(bf16[128,768]{1,0:T(8,128)(2,1)S(1)} %get-tuple-element.13), channel_id=1, source_target_pairs={{0,2},{1,3},{2,4},{3,5},{4,6},{5,7},{6,8},{7,9},{8,10},{9,11},{10,... | collective-permute-start | bytes 589832 | tf_op jit(solution)/shard_map/ppermute | solution.py:93
  35.5 1.9 %collective-permute-start.3 = (bf16[128,768]{1,0:T(8,128)(2,1)S(1)}, bf16[128,768]{1,0:T(8,128)(2,1)S(1)}, u32[]{:S(2)}, u32[]{:S(2)}) collective-permute-start(bf16[128,768]{1,0:T(8,128)(2,1)S(1)} %get-tuple-element.14), channel_id=1, source_target_pairs={{0,14},{1,15},{2,0},{3,1},{4,2},{5,3},{6,4},{7,5},{8,6},{9,7},{10,... | collective-permute-start | bytes 589832 | tf_op jit(solution)/shard_map/ppermute | solution.py:93
  37.4 0.0 copy-start
  37.4 2.9 %collective-permute-start.7 = (bf16[128,768]{1,0:T(8,128)(2,1)S(1)}, bf16[128,768]{1,0:T(8,128)(2,1)S(1)}, u32[]{:S(2)}, u32[]{:S(2)}) collective-permute-start(bf16[128,768]{1,0:T(8,128)(2,1)S(1)} %get-tuple-element.12), channel_id=1, source_target_pairs={{0,14},{1,15},{2,0},{3,1},{4,2},{5,3},{6,4},{7,5},{8,6},{9,7},{10,... | collective-permute-start | bytes 589832 | tf_op jit(solution)/shard_map/ppermute | solution.py:93
  40.3 2.3 %shard_map.76 = (bf16[1024,1024]{1,0:T(8,128)(2,1)S(1)}, bf16[64,1024]{1,0:T(8,128)(2,1)}) custom-call(bf16[128,1024]{1,0:T(8,128)(2,1)S(1)} %constant_dynamic-update-slice_fusion.3.refs_0_, bf16[128,1024]{1,0:T(8,128)(2,1)S(1)} %collective-permute-done.10.refs_1_, bf16[128,1024]{1,0:T(8,128)(2,1)S(1)} %collective-permute-done.11.refs_2_, ...), custom_call_target="tpu_custom_call" | custom-call | flops 2147483648 | tf_op jit(solution)/shard_map/pallas_call | solution.py:133
  42.7 3.4 %collective-permute-done.8.refs_7_ = bf16[128,768]{1,0:T(8,128)(2,1)S(1)} collective-permute-done((bf16[128,768]{1,0:T(8,128)(2,1)S(1)}, bf16[128,768]{1,0:T(8,128)(2,1)S(1)}, u32[]{:S(2)}, u32[]{:S(2)}) %collective-permute-start.8) | collective-permute-done | bytes 196640 | tf_op jit(solution)/shard_map/ppermute | solution.py:93
  46.1 4.3 %shard_map.77 = (bf16[64,768]{1,0:T(8,128)(2,1)}, f32[768,1024]{1,0:T(8,128)}) custom-call(bf16[64,768]{1,0:T(8,128)(2,1)S(1)} %bitcast.6, bf16[192,768]{1,0:T(8,128)(2,1)S(1)} %constant_dynamic-update-slice_fusion.refs_1_, bf16[128,768]{1,0:T(8,128)(2,1)S(1)} %collective-permute-done.3.refs_2_, bf16[128,768]{1,0:T(8,128)(2,1)S(1)} %collective-permute-done.4.refs_3_, ...), custom_call_target="tpu_custom_call" | custom-call | flops 3221225472 | tf_op jit(solution)/shard_map/pallas_call | solution.py:150
  (27 shorter events, 0.1 us)
Async XLA Ops:
  0.6 39.7 %copy-start.1 = (bf16[1024,1024]{1,0:T(8,128)(2,1)S(1)}, bf16[1024,1024]{1,0:T(8,128)(2,1)}, u32[]{:S(2)}) copy-start(bf16[1024,1024]{1,0:T(8,128)(2,1)} %refs_8_.2) | copy-start | bytes 6291460
  0.6 21.6 %collective-permute-start.2 = (bf16[64,768]{1,0:T(8,128)(2,1)}, bf16[64,768]{1,0:T(8,128)(2,1)S(1)}, u32[]{:S(2)}, u32[]{:S(2)}) collective-permute-start(bf16[64,768]{1,0:T(8,128)(2,1)} %bitcast.2), channel_id=1, source_target_pairs={{0,2},{1,3},{2,4},{3,5},{4,6},{5,7},{6,8},{7,9},{8,10},{9,11},{10,... | collective-permute-start | bytes 294920 | tf_op jit(solution)/shard_map/ppermute | solution.py:93
  3.2 13.1 %collective-permute-start.1 = (bf16[64,768]{1,0:T(8,128)(2,1)}, bf16[64,768]{1,0:T(8,128)(2,1)S(1)}, u32[]{:S(2)}, u32[]{:S(2)}) collective-permute-start(bf16[64,768]{1,0:T(8,128)(2,1)} %bitcast.3), channel_id=1, source_target_pairs={{0,8},{1,9},{2,10},{3,11},{4,12},{5,13},{6,14},{7,15},{8,0},{9,1},... | collective-permute-start | bytes 294920 | tf_op jit(solution)/shard_map/ppermute | solution.py:93
  9.2 7.0 %collective-permute-start = (bf16[64,768]{1,0:T(8,128)(2,1)}, bf16[64,768]{1,0:T(8,128)(2,1)S(1)}, u32[]{:S(2)}, u32[]{:S(2)}) collective-permute-start(bf16[64,768]{1,0:T(8,128)(2,1)} %bitcast.4), channel_id=1, source_target_pairs={{0,14},{1,15},{2,0},{3,1},{4,2},{5,3},{6,4},{7,5},{8,6},{9,7},{10,... | collective-permute-start | bytes 294920 | tf_op jit(solution)/shard_map/ppermute | solution.py:93
  11.1 5.5 %collective-permute-start.9 = (bf16[64,1024]{1,0:T(8,128)(2,1)}, bf16[64,1024]{1,0:T(8,128)(2,1)S(1)}, u32[]{:S(2)}, u32[]{:S(2)}) collective-permute-start(bf16[64,1024]{1,0:T(8,128)(2,1)} %param.7), channel_id=1, source_target_pairs={{0,128},{1,129},{2,130},{3,131},{4,132},{5,133},{6,134},{7,135},{8... | collective-permute-start | bytes 393224 | tf_op jit(solution)/shard_map/ppermute | solution.py:93
  16.7 10.7 %collective-permute-start.12 = (bf16[128,1024]{1,0:T(8,128)(2,1)S(1)}, bf16[128,1024]{1,0:T(8,128)(2,1)S(1)}, u32[]{:S(2)}, u32[]{:S(2)}) collective-permute-start(bf16[128,1024]{1,0:T(8,128)(2,1)S(1)} %constant_dynamic-update-slice_fusion.3.refs_0_), channel_id=1, source_target_pairs={{0,64},{1,65},{2,66},{3,67},{4,68},{5,69},{6,70},{7,71},{8,72},{9,... | collective-permute-start | bytes 786440 | tf_op jit(solution)/shard_map/ppermute | solution.py:93
  19.5 10.9 %collective-permute-start.11 = (bf16[128,1024]{1,0:T(8,128)(2,1)S(1)}, bf16[128,1024]{1,0:T(8,128)(2,1)S(1)}, u32[]{:S(2)}, u32[]{:S(2)}) collective-permute-start(bf16[128,1024]{1,0:T(8,128)(2,1)S(1)} %constant_dynamic-update-slice_fusion.3.refs_0_), channel_id=1, source_target_pairs={{0,32},{1,33},{2,34},{3,35},{4,36},{5,37},{6,38},{7,39},{8,40},{9,... | collective-permute-start | bytes 786440 | tf_op jit(solution)/shard_map/ppermute | solution.py:93
  19.8 12.8 %collective-permute-start.10 = (bf16[128,1024]{1,0:T(8,128)(2,1)S(1)}, bf16[128,1024]{1,0:T(8,128)(2,1)S(1)}, u32[]{:S(2)}, u32[]{:S(2)}) collective-permute-start(bf16[128,1024]{1,0:T(8,128)(2,1)S(1)} %constant_dynamic-update-slice_fusion.3.refs_0_), channel_id=1, source_target_pairs={{0,96},{1,97},{2,98},{3,99},{4,100},{5,101},{6,102},{7,103},{8,104... | collective-permute-start | bytes 786440 | tf_op jit(solution)/shard_map/ppermute | solution.py:93
  22.2 10.5 %collective-permute-start.6 = (bf16[192,768]{1,0:T(8,128)(2,1)S(1)}, bf16[192,768]{1,0:T(8,128)(2,1)S(1)}, u32[]{:S(2)}, u32[]{:S(2)}) collective-permute-start(bf16[192,768]{1,0:T(8,128)(2,1)S(1)} %constant_dynamic-update-slice_fusion.refs_1_), channel_id=1, source_target_pairs={{0,1},{1,0},{2,3},{3,2},{4,5},{5,4},{6,7},{7,6},{8,9},{9,8},{10,11... | collective-permute-start | bytes 884744 | tf_op jit(solution)/shard_map/ppermute | solution.py:93
  23.6 10.6 %collective-permute-start.13 = (bf16[128,1024]{1,0:T(8,128)(2,1)S(1)}, bf16[128,1024]{1,0:T(8,128)(2,1)S(1)}, u32[]{:S(2)}, u32[]{:S(2)}) collective-permute-start(bf16[128,1024]{1,0:T(8,128)(2,1)S(1)} %constant_dynamic-update-slice_fusion.3.refs_0_), channel_id=1, source_target_pairs={{0,16},{1,17},{2,18},{3,19},{4,20},{5,21},{6,22},{7,23},{8,24},{9,... | collective-permute-start | bytes 786440 | tf_op jit(solution)/shard_map/ppermute | solution.py:93
  27.4 8.1 %collective-permute-start.16 = (bf16[128,1024]{1,0:T(8,128)(2,1)S(1)}, bf16[128,1024]{1,0:T(8,128)(2,1)S(1)}, u32[]{:S(2)}, u32[]{:S(2)}) collective-permute-start(bf16[128,1024]{1,0:T(8,128)(2,1)S(1)} %collective-permute-done.12.refs_3_), channel_id=1, source_target_pairs={{0,16},{1,17},{2,18},{3,19},{4,20},{5,21},{6,22},{7,23},{8,24},{9,... | collective-permute-start | bytes 786440 | tf_op jit(solution)/shard_map/ppermute | solution.py:93
  30.4 6.9 %collective-permute-start.15 = (bf16[128,1024]{1,0:T(8,128)(2,1)S(1)}, bf16[128,1024]{1,0:T(8,128)(2,1)S(1)}, u32[]{:S(2)}, u32[]{:S(2)}) collective-permute-start(bf16[128,1024]{1,0:T(8,128)(2,1)S(1)} %collective-permute-done.11.refs_2_), channel_id=1, source_target_pairs={{0,16},{1,17},{2,18},{3,19},{4,20},{5,21},{6,22},{7,23},{8,24},{9,... | collective-permute-start | bytes 786440 | tf_op jit(solution)/shard_map/ppermute | solution.py:93
  32.6 4.8 %collective-permute-start.14 = (bf16[128,1024]{1,0:T(8,128)(2,1)S(1)}, bf16[128,1024]{1,0:T(8,128)(2,1)S(1)}, u32[]{:S(2)}, u32[]{:S(2)}) collective-permute-start(bf16[128,1024]{1,0:T(8,128)(2,1)S(1)} %collective-permute-done.10.refs_1_), channel_id=1, source_target_pairs={{0,16},{1,17},{2,18},{3,19},{4,20},{5,21},{6,22},{7,23},{8,24},{9,... | collective-permute-start | bytes 786440 | tf_op jit(solution)/shard_map/ppermute | solution.py:93
  32.7 9.9 %collective-permute-start.5 = (bf16[64,768]{1,0:T(8,128)(2,1)}, bf16[64,768]{1,0:T(8,128)(2,1)S(1)}, u32[]{:S(2)}, u32[]{:S(2)}) collective-permute-start(bf16[64,768]{1,0:T(8,128)(2,1)} %bitcast.5), channel_id=1, source_target_pairs={{0,1},{1,0},{2,3},{3,2},{4,5},{5,4},{6,7},{7,6},{8,9},{9,8},{10,11... | collective-permute-start | bytes 294920 | tf_op jit(solution)/shard_map/ppermute | solution.py:93
  34.2 8.5 %collective-permute-start.4 = (bf16[128,768]{1,0:T(8,128)(2,1)S(1)}, bf16[128,768]{1,0:T(8,128)(2,1)S(1)}, u32[]{:S(2)}, u32[]{:S(2)}) collective-permute-start(bf16[128,768]{1,0:T(8,128)(2,1)S(1)} %get-tuple-element.13), channel_id=1, source_target_pairs={{0,2},{1,3},{2,4},{3,5},{4,6},{5,7},{6,8},{7,9},{8,10},{9,11},{10,... | collective-permute-start | bytes 589832 | tf_op jit(solution)/shard_map/ppermute | solution.py:93
  35.5 7.2 %collective-permute-start.3 = (bf16[128,768]{1,0:T(8,128)(2,1)S(1)}, bf16[128,768]{1,0:T(8,128)(2,1)S(1)}, u32[]{:S(2)}, u32[]{:S(2)}) collective-permute-start(bf16[128,768]{1,0:T(8,128)(2,1)S(1)} %get-tuple-element.14), channel_id=1, source_target_pairs={{0,14},{1,15},{2,0},{3,1},{4,2},{5,3},{6,4},{7,5},{8,6},{9,7},{10,... | collective-permute-start | bytes 589832 | tf_op jit(solution)/shard_map/ppermute | solution.py:93
  37.4 8.7 %collective-permute-start.8 = (bf16[128,768]{1,0:T(8,128)(2,1)S(1)}, bf16[128,768]{1,0:T(8,128)(2,1)S(1)}, u32[]{:S(2)}, u32[]{:S(2)}) collective-permute-start(bf16[128,768]{1,0:T(8,128)(2,1)S(1)} %get-tuple-element.11), channel_id=1, source_target_pairs={{0,2},{1,3},{2,4},{3,5},{4,6},{5,7},{6,8},{7,9},{8,10},{9,11},{10,... | collective-permute-start | bytes 589832 | tf_op jit(solution)/shard_map/ppermute | solution.py:93
  37.4 8.7 %copy-start = (f32[768,1024]{1,0:T(8,128)S(1)}, f32[768,1024]{1,0:T(8,128)}, u32[]{:S(2)}) copy-start(f32[768,1024]{1,0:T(8,128)} %refs_10_.1) | copy-start | bytes 9437188
  37.4 8.7 %copy-start.2 = (bf16[1024,1024]{1,0:T(8,128)(2,1)S(1)}, bf16[1024,1024]{1,0:T(8,128)(2,1)}, u32[]{:S(2)}) copy-start(bf16[1024,1024]{1,0:T(8,128)(2,1)} %refs_8_.3) | copy-start | bytes 6291460
  37.4 8.7 %copy-start.3 = (bf16[768,64]{0,1:T(8,128)(2,1)S(1)}, bf16[768,64]{0,1:T(8,128)(2,1)}, u32[]{:S(2)}) copy-start(bf16[768,64]{0,1:T(8,128)(2,1)} %param.6) | copy-start | bytes 294916
  37.4 8.7 %collective-permute-start.7 = (bf16[128,768]{1,0:T(8,128)(2,1)S(1)}, bf16[128,768]{1,0:T(8,128)(2,1)S(1)}, u32[]{:S(2)}, u32[]{:S(2)}) collective-permute-start(bf16[128,768]{1,0:T(8,128)(2,1)S(1)} %get-tuple-element.12), channel_id=1, source_target_pairs={{0,14},{1,15},{2,0},{3,1},{4,2},{5,3},{6,4},{7,5},{8,6},{9,7},{10,... | collective-permute-start | bytes 589832 | tf_op jit(solution)/shard_map/ppermute | solution.py:93

commit v3 on v2

--- a/solution.py
+++ b/solution.py
@@ -88,65 +88,114 @@
         copy.wait()
 
 
+def join_kernel(pieces, *refs):
+    whole_ref, at = refs[-1], 0
+    for ref, (start, size) in zip(refs, pieces):
+        whole_ref[at : at + size, :] = ref[start : start + size, :]
+        at += size
+
+
+def join(time, *blocks):
+    blocks = [b if isinstance(b, tuple) else (b, 0, b.shape[0]) for b in blocks]
+    pieces = [b[1:] for b in blocks]
+    return pl.pallas_call(
+        functools.partial(join_kernel, pieces),
+        out_shape=jax.ShapeDtypeStruct((sum(p[1] for p in pieces), blocks[0][0].shape[1]), jnp.bfloat16),
+        in_specs=[VMEM] * len(blocks),
+        out_specs=VMEM,
+        compiler_params=pltpu.CompilerParams(vmem_limit_bytes=2 << 20),
+        cost_estimate=pl.CostEstimate(flops=int(time * 1e9), bytes_accessed=0, transcendentals=0),
+    )(*[b[0] for b in blocks])
+
+
 def on_device(trailing, column_block, row_block, lower_inv, upper_inv):
-    def send(block, target):
-        return lax.ppermute(block, ("row", "col"), pairs_of(16, 16, target))
-
-    def from_z(block, step):
-        return send(block, lambda half, x, core, z, low: (half, x, core, z - step, low))
-
-    def from_x(block, step):
-        return send(block, lambda half, x, core, z, low: (half, x - step, core, z, low))
-
-    def from_half(block):
-        return send(block, lambda half, x, core, z, low: (half ^ 1, x, core, z, low))
-
-    def from_low(block):
-        return send(block, lambda half, x, core, z, low: (half, x, core, z, low ^ 1))
-
-    def from_core(block):
-        return send(block, lambda half, x, core, z, low: (half, x, core ^ 1, z, low))
+    def send(block, name, target):
+        with jax.named_scope(name):
+            return lax.ppermute(block, ("row", "col"), pairs_of(16, 16, target))
+
+    def from_z(block, name, step):
+        return send(block, name, lambda half, x, core, z, low: (half, x, core, z - step, low))
+
+    def from_z_by_core(block, name, step):
+        return send(
+            block, name, lambda half, x, core, z, low: (half, x, core, z - (step, -step)[core], low)
+        )
+
+    def from_x(block, name, step):
+        return send(block, name, lambda half, x, core, z, low: (half, x - step, core, z, low))
+
+    def from_x_by_core(block, name, step):
+        return send(
+            block, name, lambda half, x, core, z, low: (half, x - (step, -step)[core], core, z, low)
+        )
+
+    def from_half(block, name):
+        return send(block, name, lambda half, x, core, z, low: (half ^ 1, x, core, z, low))
+
+    def from_low(block, name):
+        return send(block, name, lambda half, x, core, z, low: (half, x, core, z, low ^ 1))
+
+    def from_core(block, name):
+        return send(block, name, lambda half, x, core, z, low: (half, x, core ^ 1, z, low))
+
+    def after(block, *others):
+        return lax.optimization_barrier((block, *others))[0] if others else block
 
     rows, cols = trailing.shape
     nb = upper_inv.shape[0]
     share = column_block.shape[1]
     own_a, own_b = column_block.T, row_block
 
-    a_next, a_prev = from_z(own_a, 1), from_z(own_a, -1)
-    other_half = from_half(own_b)
-    a_far = from_z(own_a, 4)
-    other_low = from_low(own_a)
-
-    b_x = [jnp.concatenate([own_b, other_half], 0)]
-    b_x += [from_x(b_x[0], step) for step in (1, 3, 2)]
-    b_core = [from_core(block) for block in b_x]
-
-    three = jnp.concatenate([a_next, a_far, a_prev], 0)
-    up = from_z(three[: 2 * share], 1)
-    down = from_z(three[share:], -1)
-    low_three = from_low(three)
-    low_up = from_z(low_three[: 2 * share], 1)
-    low_down = from_z(low_three[share:], -1)
-
-    steps = (0, 1, 3, 2)
-    b_places = [[(dx, dhalf, dcore) for dhalf in (0, 1)] for dcore in (0, 1) for dx in steps]
+    half_b = from_half(own_b, "half")
+    a_next = from_z(own_a, "next", 1)
+    a_prev = from_z(own_a, "prev", -1)
+    a_far = from_z(own_a, "far", 4)
+    b_two = join(0.3, own_b, half_b)
+    pair = join(0.6, a_next, a_prev)
+    low_pair = from_low(pair, "low_pair")
+    b_x1 = from_x(b_two, "x1", 1)
+    b_x3 = from_x(b_two, "x3", 3)
+    b_c0 = from_core(b_two, "c0")
+    b_x2 = from_x(b_two, "x2", 2)
+    low_own = from_low(after(own_a, low_pair), "low_own")
+    low_far = from_low(a_far, "low_far")
+    for_up = join(0, a_next, a_far)
+    for_down = join(0, a_far, a_prev)
+    up = from_z(for_up, "up", 1)
+    down = from_z(for_down, "down", -1)
+    b_c1 = from_core(b_x1, "c1")
+    b_c2 = from_core(b_x3, "c2")
+    for_low_up = join(1, (low_pair, 0, share), low_far)
+    for_low_down = join(1, low_far, (low_pair, share, share))
+    low_up = from_z(for_low_up, "lup", 1)
+    low_down = from_z(for_low_down, "ldn", -1)
+    b_c3 = from_core(b_x2, "c3")
+    low_last = join(4, low_up, low_down)
+
+    b_pieces = [b_two, b_x1, b_x3, b_x2, b_c0, b_c1, b_c2, b_c3]
+    b_places = [[(dx, dhalf, dcore) for dhalf in (0, 1)] for dcore in (0, 1) for dx in (0, 1, 3, 2)]
+    a_pieces = [own_a, pair, a_far, up, down, low_own, low_pair, low_far, low_last]
+    a_places = [
+        [(dz, dlow) for dz in steps]
+        for dlow, steps in (
+            (0, (0,)), (0, (1, 7)), (0, (4,)), (0, (2, 5)), (0, (3, 6)),
+            (1, (0,)), (1, (1, 7)), (1, (4,)), (1, (2, 5, 3, 6)),
+        )
+    ]
+
     upper_full, upper_tile = pl.pallas_call(
         functools.partial(upper_kernel, b_places),
         out_shape=[
             jax.ShapeDtypeStruct((nb, cols), jnp.bfloat16),
             jax.ShapeDtypeStruct(row_block.shape, jnp.bfloat16),
         ],
-        in_specs=[VMEM] * 9,
+        in_specs=[VMEM] * (len(b_pieces) + 1),
         out_specs=[VMEM, HBM],
         scratch_shapes=[pltpu.VMEM((nb, cols), jnp.bfloat16), pltpu.SemaphoreType.DMA],
         compiler_params=pltpu.CompilerParams(vmem_limit_bytes=8 << 20),
-        cost_estimate=pl.CostEstimate(flops=2 * nb * nb * cols, bytes_accessed=0, transcendentals=0),
-    )(*b_x, *b_core, lower_inv)
-
-    a_places = [
-        [(0, 0)], [(1, 0), (4, 0), (7, 0)], [(2, 0), (5, 0)], [(3, 0), (6, 0)],
-        [(0, 1)], [(1, 1), (4, 1), (7, 1)], [(2, 1), (5, 1)], [(3, 1), (6, 1)],
-    ]
+        cost_estimate=pl.CostEstimate(flops=0, bytes_accessed=0, transcendentals=0),
+    )(*b_pieces, lower_inv)
+
     lower_tile, updated = pl.pallas_call(
         functools.partial(update_kernel, a_places),
         out_shape=[
@@ -164,7 +213,7 @@
         ],
         compiler_params=pltpu.CompilerParams(vmem_limit_bytes=12 << 20),
         cost_estimate=pl.CostEstimate(flops=2 * rows * nb * (nb + cols), bytes_accessed=0, transcendentals=0),
-    )(own_a, three, up, down, other_low, low_three, low_up, low_down, upper_inv, upper_full, trailing)
+    )(*a_pieces, upper_inv, upper_full, trailing)
     return lower_tile.T, upper_tile, updated
 
 

time: 50.6 us -> 47.2 us (0.933)
  starting transfers between devices: 36.3 us -> 34 us
  local copies, waits for them, and re-layouts: 1.03 us -> 0.03 us
    ppermute x17 -> x18, starting transfers between devices: 36.3 us -> 34 us  [send(): return lax.ppermute(block, ('row', 'col'), pairs_of(16, 16, target))]
    unnamed x11 -> x10, local copies, waits for them, and re-layouts: 0.99 us -> 0.03 us
    ppermute x17 -> x18, waiting for transfers between devices: 5.63 us -> 5.43 us  [send(): return lax.ppermute(block, ('row', 'col'), pairs_of(16, 16, target))]
  transfers between devices with their start and end apart: 17 -> 18, of which waited for: 4 -> 5; matrix products, arithmetic and copies ran while one was open for 2% -> 0% of each run, Pallas kernels for 5% -> 5%
where the time goes in v3:
time: 47.2 us; the launch traced here: 47.1 us
  starting transfers between devices  34 us (72%)
  Pallas kernels  6.72 us (14%)
  waiting for transfers between devices  5.43 us (12%)
  between operations  0.93 us (2%)
    ppermute x18, starting transfers between devices, send(): return lax.ppermute(block, ('row', 'col'), pairs_of(16, 16, target))  34 us
    ppermute x18, waiting for transfers between devices, send(): return lax.ppermute(block, ('row', 'col'), pairs_of(16, 16, target))  5.43 us
    pallas_call x1, Pallas kernels, on_device(): pl.pallas_call(functools.partial(update_kernel, a_places), out_shape=[jax...  4.27 us
    pallas_call x1, Pallas kernels, on_device(): pl.pallas_call(functools.partial(upper_kernel, b_places), out_shape=[jax....  2.34 us
  transfers between devices with their start and end apart: 18, of which 5 were waited for; matrix products, arithmetic and copies ran while one was open for 0% of the time, Pallas kernels for 5%

profile of v3, /device:TPU:1, one launch (start us, length us, event | category | flops | bytes accessed | tf_op | source)
XLA Modules:
  0.0 47.1 jit_solution(5166419555948074545)
XLA Ops:
  0.6 2.5 %collective-permute-start.1 = (bf16[64,768]{1,0:T(8,128)(2,1)}, bf16[64,768]{1,0:T(8,128)(2,1)S(1)}, u32[]{:S(2)}, u32[]{:S(2)}) collective-permute-start(bf16[64,768]{1,0:T(8,128)(2,1)} %bitcast.2), channel_id=1, source_target_pairs={{0,2},{1,3},{2,4},{3,5},{4,6},{5,7},{6,8},{7,9},{8,10},{9,11},{10,... | collective-permute-start | bytes 294920 | tf_op jit(solution)/shard_map/prev/ppermute | solution.py:114
  3.2 4.0 %collective-permute-start = (bf16[64,768]{1,0:T(8,128)(2,1)}, bf16[64,768]{1,0:T(8,128)(2,1)S(1)}, u32[]{:S(2)}, u32[]{:S(2)}) collective-permute-start(bf16[64,768]{1,0:T(8,128)(2,1)} %bitcast.3), channel_id=1, source_target_pairs={{0,14},{1,15},{2,0},{3,1},{4,2},{5,3},{6,4},{7,5},{8,6},{9,7},{10,... | collective-permute-start | bytes 294920 | tf_op jit(solution)/shard_map/next/ppermute | solution.py:114
  7.2 2.9 %collective-permute-start.10 = (bf16[64,1024]{1,0:T(8,128)(2,1)}, bf16[64,1024]{1,0:T(8,128)(2,1)S(1)}, u32[]{:S(2)}, u32[]{:S(2)}) collective-permute-start(bf16[64,1024]{1,0:T(8,128)(2,1)} %refs_0_.1), channel_id=1, source_target_pairs={{0,128},{1,129},{2,130},{3,131},{4,132},{5,133},{6,134},{7,135},{8... | collective-permute-start | bytes 393224 | tf_op jit(solution)/shard_map/half/ppermute | solution.py:114
  10.1 3.9 %collective-permute-start.2 = (bf16[64,768]{1,0:T(8,128)(2,1)}, bf16[64,768]{1,0:T(8,128)(2,1)S(1)}, u32[]{:S(2)}, u32[]{:S(2)}) collective-permute-start(bf16[64,768]{1,0:T(8,128)(2,1)} %bitcast.4), channel_id=1, source_target_pairs={{0,8},{1,9},{2,10},{3,11},{4,12},{5,13},{6,14},{7,15},{8,0},{9,1},... | collective-permute-start | bytes 294920 | tf_op jit(solution)/shard_map/far/ppermute | solution.py:114
  14.1 0.5 %collective-permute-start.5 = (bf16[128,768]{1,0:T(8,128)(2,1)S(1)}, bf16[128,768]{1,0:T(8,128)(2,1)S(1)}, u32[]{:S(2)}, u32[]{:S(2)}) collective-permute-start(bf16[128,768]{1,0:T(8,128)(2,1)S(1)} %shard_map.76.refs_1_), channel_id=1, source_target_pairs={{0,1},{1,0},{2,3},{3,2},{4,5},{5,4},{6,7},{7,6},{8,9},{9,8},{10,11... | collective-permute-start | bytes 589832 | tf_op jit(solution)/shard_map/low_pair/ppermute | solution.py:114
  14.6 2.8 %collective-permute-start.13 = (bf16[128,1024]{1,0:T(8,128)(2,1)S(1)}, bf16[128,1024]{1,0:T(8,128)(2,1)S(1)}, u32[]{:S(2)}, u32[]{:S(2)}) collective-permute-start(bf16[128,1024]{1,0:T(8,128)(2,1)S(1)} %shard_map.82.refs_0_), channel_id=1, source_target_pairs={{0,64},{1,65},{2,66},{3,67},{4,68},{5,69},{6,70},{7,71},{8,72},{9,... | collective-permute-start | bytes 786440 | tf_op jit(solution)/shard_map/x2/ppermute | solution.py:114
  17.4 0.3 collective-permute-done.2.refs_1_.refs_0_.refs_2_
  17.7 0.8 %collective-permute-start.7 = (bf16[64,768]{1,0:T(8,128)(2,1)S(1)}, bf16[64,768]{1,0:T(8,128)(2,1)S(1)}, u32[]{:S(2)}, u32[]{:S(2)}) collective-permute-start(bf16[64,768]{1,0:T(8,128)(2,1)S(1)} %collective-permute-done.2.refs_1_.refs_0_.refs_2_), channel_id=1, source_target_pairs={{0,1},{1,0},{2,3},{3,2},{4,5},{5,4},{6,7},{7,6},{8,9},{9,8},{10,11... | collective-permute-start | bytes 294920 | tf_op jit(solution)/shard_map/low_far/ppermute | solution.py:114
  18.5 4.2 %collective-permute-start.14 = (bf16[128,1024]{1,0:T(8,128)(2,1)S(1)}, bf16[128,1024]{1,0:T(8,128)(2,1)S(1)}, u32[]{:S(2)}, u32[]{:S(2)}) collective-permute-start(bf16[128,1024]{1,0:T(8,128)(2,1)S(1)} %shard_map.82.refs_0_), channel_id=1, source_target_pairs={{0,16},{1,17},{2,18},{3,19},{4,20},{5,21},{6,22},{7,23},{8,24},{9,... | collective-permute-start | bytes 786440 | tf_op jit(solution)/shard_map/c0/ppermute | solution.py:114
  22.7 1.2 %collective-permute-start.12 = (bf16[128,1024]{1,0:T(8,128)(2,1)S(1)}, bf16[128,1024]{1,0:T(8,128)(2,1)S(1)}, u32[]{:S(2)}, u32[]{:S(2)}) collective-permute-start(bf16[128,1024]{1,0:T(8,128)(2,1)S(1)} %shard_map.82.refs_0_), channel_id=1, source_target_pairs={{0,32},{1,33},{2,34},{3,35},{4,36},{5,37},{6,38},{7,39},{8,40},{9,... | collective-permute-start | bytes 786440 | tf_op jit(solution)/shard_map/x3/ppermute | solution.py:114
  23.9 1.5 %collective-permute-start.11 = (bf16[128,1024]{1,0:T(8,128)(2,1)S(1)}, bf16[128,1024]{1,0:T(8,128)(2,1)S(1)}, u32[]{:S(2)}, u32[]{:S(2)}) collective-permute-start(bf16[128,1024]{1,0:T(8,128)(2,1)S(1)} %shard_map.82.refs_0_), channel_id=1, source_target_pairs={{0,96},{1,97},{2,98},{3,99},{4,100},{5,101},{6,102},{7,103},{8,104... | collective-permute-start | bytes 786440 | tf_op jit(solution)/shard_map/x1/ppermute | solution.py:114
  25.4 1.4 %collective-permute-start.8 = (bf16[128,768]{1,0:T(8,128)(2,1)S(1)}, bf16[128,768]{1,0:T(8,128)(2,1)S(1)}, u32[]{:S(2)}, u32[]{:S(2)}) collective-permute-start(bf16[128,768]{1,0:T(8,128)(2,1)S(1)} %shard_map.79), channel_id=1, source_target_pairs={{0,14},{1,15},{2,0},{3,1},{4,2},{5,3},{6,4},{7,5},{8,6},{9,7},{10,... | collective-permute-start | bytes 589832 | tf_op jit(solution)/shard_map/lup/ppermute | solution.py:114
  26.9 2.9 %collective-permute-start.17 = (bf16[128,1024]{1,0:T(8,128)(2,1)S(1)}, bf16[128,1024]{1,0:T(8,128)(2,1)S(1)}, u32[]{:S(2)}, u32[]{:S(2)}) collective-permute-start(bf16[128,1024]{1,0:T(8,128)(2,1)S(1)} %collective-permute-done.13.refs_3_), channel_id=1, source_target_pairs={{0,16},{1,17},{2,18},{3,19},{4,20},{5,21},{6,22},{7,23},{8,24},{9,... | collective-permute-start | bytes 786440 | tf_op jit(solution)/shard_map/c3/ppermute | solution.py:114
  29.8 1.6 %collective-permute-start.9 = (bf16[128,768]{1,0:T(8,128)(2,1)S(1)}, bf16[128,768]{1,0:T(8,128)(2,1)S(1)}, u32[]{:S(2)}, u32[]{:S(2)}) collective-permute-start(bf16[128,768]{1,0:T(8,128)(2,1)S(1)} %shard_map.80), channel_id=1, source_target_pairs={{0,2},{1,3},{2,4},{3,5},{4,6},{5,7},{6,8},{7,9},{8,10},{9,11},{10,... | collective-permute-start | bytes 589832 | tf_op jit(solution)/shard_map/ldn/ppermute | solution.py:114
  31.4 0.4 collective-permute-done.12.refs_2_
  31.9 0.8 %collective-permute-start.3 = (bf16[128,768]{1,0:T(8,128)(2,1)S(1)}, bf16[128,768]{1,0:T(8,128)(2,1)S(1)}, u32[]{:S(2)}, u32[]{:S(2)}) collective-permute-start(bf16[128,768]{1,0:T(8,128)(2,1)S(1)} %shard_map.77), channel_id=1, source_target_pairs={{0,14},{1,15},{2,0},{3,1},{4,2},{5,3},{6,4},{7,5},{8,6},{9,7},{10,... | collective-permute-start | bytes 589832 | tf_op jit(solution)/shard_map/up/ppermute | solution.py:114
  32.7 0.7 %collective-permute-start.4 = (bf16[128,768]{1,0:T(8,128)(2,1)S(1)}, bf16[128,768]{1,0:T(8,128)(2,1)S(1)}, u32[]{:S(2)}, u32[]{:S(2)}) collective-permute-start(bf16[128,768]{1,0:T(8,128)(2,1)S(1)} %shard_map.78), channel_id=1, source_target_pairs={{0,2},{1,3},{2,4},{3,5},{4,6},{5,7},{6,8},{7,9},{8,10},{9,11},{10,... | collective-permute-start | bytes 589832 | tf_op jit(solution)/shard_map/down/ppermute | solution.py:114
  33.3 1.1 %collective-permute-start.6 = (bf16[64,768]{1,0:T(8,128)(2,1)S(1)}, bf16[64,768]{1,0:T(8,128)(2,1)S(1)}, u32[]{:S(2)}, u32[]{:S(2)}) collective-permute-start(bf16[64,768]{1,0:T(8,128)(2,1)S(1)} %bitcast.5), channel_id=1, source_target_pairs={{0,1},{1,0},{2,3},{3,2},{4,5},{5,4},{6,7},{7,6},{8,9},{9,8},{10,11... | collective-permute-start | bytes 294920 | tf_op jit(solution)/shard_map/low_own/ppermute | solution.py:114
  34.4 3.2 %collective-permute-done.9.refs_1_ = bf16[128,768]{1,0:T(8,128)(2,1)S(1)} collective-permute-done((bf16[128,768]{1,0:T(8,128)(2,1)S(1)}, bf16[128,768]{1,0:T(8,128)(2,1)S(1)}, u32[]{:S(2)}, u32[]{:S(2)}) %collective-permute-start.9) | collective-permute-done | bytes 196640 | tf_op jit(solution)/shard_map/ldn/ppermute | solution.py:114
  37.6 1.2 %collective-permute-start.16 = (bf16[128,1024]{1,0:T(8,128)(2,1)S(1)}, bf16[128,1024]{1,0:T(8,128)(2,1)S(1)}, u32[]{:S(2)}, u32[]{:S(2)}) collective-permute-start(bf16[128,1024]{1,0:T(8,128)(2,1)S(1)} %collective-permute-done.12.refs_2_), channel_id=1, source_target_pairs={{0,16},{1,17},{2,18},{3,19},{4,20},{5,21},{6,22},{7,23},{8,24},{9,... | collective-permute-start | bytes 786440 | tf_op jit(solution)/shard_map/c2/ppermute | solution.py:114
  38.8 1.1 %collective-permute-done.16.refs_6_ = bf16[128,1024]{1,0:T(8,128)(2,1)S(1)} collective-permute-done((bf16[128,1024]{1,0:T(8,128)(2,1)S(1)}, bf16[128,1024]{1,0:T(8,128)(2,1)S(1)}, u32[]{:S(2)}, u32[]{:S(2)}) %collective-permute-start.16) | collective-permute-done | bytes 262176 | tf_op jit(solution)/shard_map/c2/ppermute | solution.py:114
  39.9 0.4 collective-permute-done.15.refs_5_
  40.3 2.3 %shard_map.83 = (bf16[1024,1024]{1,0:T(8,128)(2,1)S(1)}, bf16[64,1024]{1,0:T(8,128)(2,1)}) custom-call(bf16[128,1024]{1,0:T(8,128)(2,1)S(1)} %shard_map.82.refs_0_, bf16[128,1024]{1,0:T(8,128)(2,1)S(1)} %collective-permute-done.11.refs_1_, bf16[128,1024]{1,0:T(8,128)(2,1)S(1)} %collective-permute-done.12.refs_2_, ...), custom_call_target="tpu_custom_call" | custom-call | tf_op jit(solution)/shard_map/pallas_call | solution.py:186
  42.7 4.3 %shard_map.84 = (bf16[64,768]{1,0:T(8,128)(2,1)}, f32[768,1024]{1,0:T(8,128)}) custom-call(bf16[64,768]{1,0:T(8,128)(2,1)S(1)} %bitcast.6, bf16[128,768]{1,0:T(8,128)(2,1)S(1)} %shard_map.76.refs_1_, bf16[64,768]{1,0:T(8,128)(2,1)S(1)} %collective-permute-done.2.refs_1_.refs_0_.refs_2_, bf16[128,768]{1,0:T(8,128)(2,1)S(1)} %collective-permute-done.3.refs_3_, ...), custom_call_target="tpu_custom_call" | custom-call | flops 3221225472 | tf_op jit(solution)/shard_map/pallas_call | solution.py:199
  (31 shorter events, 0.2 us)
Async XLA Ops:
  0.6 13.9 %copy-start.3 = (bf16[64,1024]{1,0:T(8,128)(2,1)S(1)}, bf16[64,1024]{1,0:T(8,128)(2,1)}, u32[]{:S(2)}) copy-start(bf16[64,1024]{1,0:T(8,128)(2,1)} %refs_0_.1) | copy-start | bytes 393220
  0.6 13.4 %collective-permute-start.1 = (bf16[64,768]{1,0:T(8,128)(2,1)}, bf16[64,768]{1,0:T(8,128)(2,1)S(1)}, u32[]{:S(2)}, u32[]{:S(2)}) collective-permute-start(bf16[64,768]{1,0:T(8,128)(2,1)} %bitcast.2), channel_id=1, source_target_pairs={{0,2},{1,3},{2,4},{3,5},{4,6},{5,7},{6,8},{7,9},{8,10},{9,11},{10,... | collective-permute-start | bytes 294920 | tf_op jit(solution)/shard_map/prev/ppermute | solution.py:114
  3.2 10.9 %collective-permute-start = (bf16[64,768]{1,0:T(8,128)(2,1)}, bf16[64,768]{1,0:T(8,128)(2,1)S(1)}, u32[]{:S(2)}, u32[]{:S(2)}) collective-permute-start(bf16[64,768]{1,0:T(8,128)(2,1)} %bitcast.3), channel_id=1, source_target_pairs={{0,14},{1,15},{2,0},{3,1},{4,2},{5,3},{6,4},{7,5},{8,6},{9,7},{10,... | collective-permute-start | bytes 294920 | tf_op jit(solution)/shard_map/next/ppermute | solution.py:114
  7.2 7.3 %collective-permute-start.10 = (bf16[64,1024]{1,0:T(8,128)(2,1)}, bf16[64,1024]{1,0:T(8,128)(2,1)S(1)}, u32[]{:S(2)}, u32[]{:S(2)}) collective-permute-start(bf16[64,1024]{1,0:T(8,128)(2,1)} %refs_0_.1), channel_id=1, source_target_pairs={{0,128},{1,129},{2,130},{3,131},{4,132},{5,133},{6,134},{7,135},{8... | collective-permute-start | bytes 393224 | tf_op jit(solution)/shard_map/half/ppermute | solution.py:114
  10.1 7.6 %collective-permute-start.2 = (bf16[64,768]{1,0:T(8,128)(2,1)}, bf16[64,768]{1,0:T(8,128)(2,1)S(1)}, u32[]{:S(2)}, u32[]{:S(2)}) collective-permute-start(bf16[64,768]{1,0:T(8,128)(2,1)} %bitcast.4), channel_id=1, source_target_pairs={{0,8},{1,9},{2,10},{3,11},{4,12},{5,13},{6,14},{7,15},{8,0},{9,1},... | collective-permute-start | bytes 294920 | tf_op jit(solution)/shard_map/far/ppermute | solution.py:114
  14.1 11.3 %collective-permute-start.5 = (bf16[128,768]{1,0:T(8,128)(2,1)S(1)}, bf16[128,768]{1,0:T(8,128)(2,1)S(1)}, u32[]{:S(2)}, u32[]{:S(2)}) collective-permute-start(bf16[128,768]{1,0:T(8,128)(2,1)S(1)} %shard_map.76.refs_1_), channel_id=1, source_target_pairs={{0,1},{1,0},{2,3},{3,2},{4,5},{5,4},{6,7},{7,6},{8,9},{9,8},{10,11... | collective-permute-start | bytes 589832 | tf_op jit(solution)/shard_map/low_pair/ppermute | solution.py:114
  14.6 12.3 %collective-permute-start.13 = (bf16[128,1024]{1,0:T(8,128)(2,1)S(1)}, bf16[128,1024]{1,0:T(8,128)(2,1)S(1)}, u32[]{:S(2)}, u32[]{:S(2)}) collective-permute-start(bf16[128,1024]{1,0:T(8,128)(2,1)S(1)} %shard_map.82.refs_0_), channel_id=1, source_target_pairs={{0,64},{1,65},{2,66},{3,67},{4,68},{5,69},{6,70},{7,71},{8,72},{9,... | collective-permute-start | bytes 786440 | tf_op jit(solution)/shard_map/x2/ppermute | solution.py:114
  17.7 6.2 %collective-permute-start.7 = (bf16[64,768]{1,0:T(8,128)(2,1)S(1)}, bf16[64,768]{1,0:T(8,128)(2,1)S(1)}, u32[]{:S(2)}, u32[]{:S(2)}) collective-permute-start(bf16[64,768]{1,0:T(8,128)(2,1)S(1)} %collective-permute-done.2.refs_1_.refs_0_.refs_2_), channel_id=1, source_target_pairs={{0,1},{1,0},{2,3},{3,2},{4,5},{5,4},{6,7},{7,6},{8,9},{9,8},{10,11... | collective-permute-start | bytes 294920 | tf_op jit(solution)/shard_map/low_far/ppermute | solution.py:114
  18.5 11.3 %collective-permute-start.14 = (bf16[128,1024]{1,0:T(8,128)(2,1)S(1)}, bf16[128,1024]{1,0:T(8,128)(2,1)S(1)}, u32[]{:S(2)}, u32[]{:S(2)}) collective-permute-start(bf16[128,1024]{1,0:T(8,128)(2,1)S(1)} %shard_map.82.refs_0_), channel_id=1, source_target_pairs={{0,16},{1,17},{2,18},{3,19},{4,20},{5,21},{6,22},{7,23},{8,24},{9,... | collective-permute-start | bytes 786440 | tf_op jit(solution)/shard_map/c0/ppermute | solution.py:114
  22.7 9.1 %collective-permute-start.12 = (bf16[128,1024]{1,0:T(8,128)(2,1)S(1)}, bf16[128,1024]{1,0:T(8,128)(2,1)S(1)}, u32[]{:S(2)}, u32[]{:S(2)}) collective-permute-start(bf16[128,1024]{1,0:T(8,128)(2,1)S(1)} %shard_map.82.refs_0_), channel_id=1, source_target_pairs={{0,32},{1,33},{2,34},{3,35},{4,36},{5,37},{6,38},{7,39},{8,40},{9,... | collective-permute-start | bytes 786440 | tf_op jit(solution)/shard_map/x3/ppermute | solution.py:114
  23.9 8.7 %collective-permute-start.11 = (bf16[128,1024]{1,0:T(8,128)(2,1)S(1)}, bf16[128,1024]{1,0:T(8,128)(2,1)S(1)}, u32[]{:S(2)}, u32[]{:S(2)}) collective-permute-start(bf16[128,1024]{1,0:T(8,128)(2,1)S(1)} %shard_map.82.refs_0_), channel_id=1, source_target_pairs={{0,96},{1,97},{2,98},{3,99},{4,100},{5,101},{6,102},{7,103},{8,104... | collective-permute-start | bytes 786440 | tf_op jit(solution)/shard_map/x1/ppermute | solution.py:114
  25.4 7.9 %copy-start.4 = (bf16[768,64]{0,1:T(8,128)(2,1)S(1)}, bf16[768,64]{0,1:T(8,128)(2,1)}, u32[]{:S(2)}) copy-start(bf16[768,64]{0,1:T(8,128)(2,1)} %param.6) | copy-start | bytes 294916
  25.4 7.9 %collective-permute-start.8 = (bf16[128,768]{1,0:T(8,128)(2,1)S(1)}, bf16[128,768]{1,0:T(8,128)(2,1)S(1)}, u32[]{:S(2)}, u32[]{:S(2)}) collective-permute-start(bf16[128,768]{1,0:T(8,128)(2,1)S(1)} %shard_map.79), channel_id=1, source_target_pairs={{0,14},{1,15},{2,0},{3,1},{4,2},{5,3},{6,4},{7,5},{8,6},{9,7},{10,... | collective-permute-start | bytes 589832 | tf_op jit(solution)/shard_map/lup/ppermute | solution.py:114
  26.9 11.9 %collective-permute-start.17 = (bf16[128,1024]{1,0:T(8,128)(2,1)S(1)}, bf16[128,1024]{1,0:T(8,128)(2,1)S(1)}, u32[]{:S(2)}, u32[]{:S(2)}) collective-permute-start(bf16[128,1024]{1,0:T(8,128)(2,1)S(1)} %collective-permute-done.13.refs_3_), channel_id=1, source_target_pairs={{0,16},{1,17},{2,18},{3,19},{4,20},{5,21},{6,22},{7,23},{8,24},{9,... | collective-permute-start | bytes 786440 | tf_op jit(solution)/shard_map/c3/ppermute | solution.py:114
  29.8 7.8 %collective-permute-start.9 = (bf16[128,768]{1,0:T(8,128)(2,1)S(1)}, bf16[128,768]{1,0:T(8,128)(2,1)S(1)}, u32[]{:S(2)}, u32[]{:S(2)}) collective-permute-start(bf16[128,768]{1,0:T(8,128)(2,1)S(1)} %shard_map.80), channel_id=1, source_target_pairs={{0,2},{1,3},{2,4},{3,5},{4,6},{5,7},{6,8},{7,9},{8,10},{9,11},{10,... | collective-permute-start | bytes 589832 | tf_op jit(solution)/shard_map/ldn/ppermute | solution.py:114
  31.4 8.9 %copy-start = (bf16[1024,1024]{1,0:T(8,128)(2,1)S(1)}, bf16[1024,1024]{1,0:T(8,128)(2,1)}, u32[]{:S(2)}) copy-start(bf16[1024,1024]{1,0:T(8,128)(2,1)} %refs_8_.1) | copy-start | bytes 6291460
  31.9 10.8 %collective-permute-start.3 = (bf16[128,768]{1,0:T(8,128)(2,1)S(1)}, bf16[128,768]{1,0:T(8,128)(2,1)S(1)}, u32[]{:S(2)}, u32[]{:S(2)}) collective-permute-start(bf16[128,768]{1,0:T(8,128)(2,1)S(1)} %shard_map.77), channel_id=1, source_target_pairs={{0,14},{1,15},{2,0},{3,1},{4,2},{5,3},{6,4},{7,5},{8,6},{9,7},{10,... | collective-permute-start | bytes 589832 | tf_op jit(solution)/shard_map/up/ppermute | solution.py:114
  32.7 10.0 %collective-permute-start.4 = (bf16[128,768]{1,0:T(8,128)(2,1)S(1)}, bf16[128,768]{1,0:T(8,128)(2,1)S(1)}, u32[]{:S(2)}, u32[]{:S(2)}) collective-permute-start(bf16[128,768]{1,0:T(8,128)(2,1)S(1)} %shard_map.78), channel_id=1, source_target_pairs={{0,2},{1,3},{2,4},{3,5},{4,6},{5,7},{6,8},{7,9},{8,10},{9,11},{10,... | collective-permute-start | bytes 589832 | tf_op jit(solution)/shard_map/down/ppermute | solution.py:114
  33.3 9.3 %collective-permute-start.6 = (bf16[64,768]{1,0:T(8,128)(2,1)S(1)}, bf16[64,768]{1,0:T(8,128)(2,1)S(1)}, u32[]{:S(2)}, u32[]{:S(2)}) collective-permute-start(bf16[64,768]{1,0:T(8,128)(2,1)S(1)} %bitcast.5), channel_id=1, source_target_pairs={{0,1},{1,0},{2,3},{3,2},{4,5},{5,4},{6,7},{7,6},{8,9},{9,8},{10,11... | collective-permute-start | bytes 294920 | tf_op jit(solution)/shard_map/low_own/ppermute | solution.py:114
  37.6 2.3 %collective-permute-start.16 = (bf16[128,1024]{1,0:T(8,128)(2,1)S(1)}, bf16[128,1024]{1,0:T(8,128)(2,1)S(1)}, u32[]{:S(2)}, u32[]{:S(2)}) collective-permute-start(bf16[128,1024]{1,0:T(8,128)(2,1)S(1)} %collective-permute-done.12.refs_2_), channel_id=1, source_target_pairs={{0,16},{1,17},{2,18},{3,19},{4,20},{5,21},{6,22},{7,23},{8,24},{9,... | collective-permute-start | bytes 786440 | tf_op jit(solution)/shard_map/c2/ppermute | solution.py:114
  38.8 1.5 %collective-permute-start.15 = (bf16[128,1024]{1,0:T(8,128)(2,1)S(1)}, bf16[128,1024]{1,0:T(8,128)(2,1)S(1)}, u32[]{:S(2)}, u32[]{:S(2)}) collective-permute-start(bf16[128,1024]{1,0:T(8,128)(2,1)S(1)} %collective-permute-done.11.refs_1_), channel_id=1, source_target_pairs={{0,16},{1,17},{2,18},{3,19},{4,20},{5,21},{6,22},{7,23},{8,24},{9,... | collective-permute-start | bytes 786440 | tf_op jit(solution)/shard_map/c1/ppermute | solution.py:114
  38.8 3.9 %copy-start.2 = (bf16[1024,1024]{1,0:T(8,128)(2,1)S(1)}, bf16[1024,1024]{1,0:T(8,128)(2,1)}, u32[]{:S(2)}) copy-start(bf16[1024,1024]{1,0:T(8,128)(2,1)} %refs_9_.1) | copy-start | bytes 6291460
  38.8 3.9 %copy-start.1 = (f32[768,1024]{1,0:T(8,128)S(1)}, f32[768,1024]{1,0:T(8,128)}, u32[]{:S(2)}) copy-start(f32[768,1024]{1,0:T(8,128)} %refs_11_.1) | copy-start | bytes 9437188

commit v4 on v3

--- a/solution.py
+++ b/solution.py
@@ -157,7 +157,6 @@
     b_x3 = from_x(b_two, "x3", 3)
     b_c0 = from_core(b_two, "c0")
     b_x2 = from_x(b_two, "x2", 2)
-    low_own = from_low(after(own_a, low_pair), "low_own")
     low_far = from_low(a_far, "low_far")
     for_up = join(0, a_next, a_far)
     for_down = join(0, a_far, a_prev)
@@ -165,6 +164,7 @@
     down = from_z(for_down, "down", -1)
     b_c1 = from_core(b_x1, "c1")
     b_c2 = from_core(b_x3, "c2")
+    low_own = from_low(after(own_a, b_c1, b_c2), "low_own")
     for_low_up = join(1, (low_pair, 0, share), low_far)
     for_low_down = join(1, low_far, (low_pair, share, share))
     low_up = from_z(for_low_up, "lup", 1)

time: 47.2 us -> 45.3 us (0.960)
  the two profiles are of different devices: /device:TPU:1 before, /device:TPU:30 now
where the time goes in v4:
time: 45.3 us; the launch traced here: 45.2 us
  starting transfers between devices  19.8 us (44%)
  waiting for transfers between devices  17.6 us (39%)
  Pallas kernels  6.73 us (15%)
  between operations  0.97 us (2%)
    ppermute x18, starting transfers between devices, send(): return lax.ppermute(block, ('row', 'col'), pairs_of(16, 16, target))  19.8 us
    ppermute x18, waiting for transfers between devices, send(): return lax.ppermute(block, ('row', 'col'), pairs_of(16, 16, target))  17.6 us
    pallas_call x1, Pallas kernels, on_device(): pl.pallas_call(functools.partial(update_kernel, a_places), out_shape=[jax...  4.27 us
    pallas_call x1, Pallas kernels, on_device(): pl.pallas_call(functools.partial(upper_kernel, b_places), out_shape=[jax....  2.34 us
  transfers between devices with their start and end apart: 18, of which 7 were waited for; matrix products, arithmetic and copies ran while one was open for 0% of the time, Pallas kernels for 5%

profile of v4, /device:TPU:30, one launch (start us, length us, event | category | flops | bytes accessed | tf_op | source)
XLA Modules:
  0.0 45.2 jit_solution(10308495588315507657)
XLA Ops:
  0.6 2.0 %collective-permute-start.1 = (bf16[64,768]{1,0:T(8,128)(2,1)}, bf16[64,768]{1,0:T(8,128)(2,1)S(1)}, u32[]{:S(2)}, u32[]{:S(2)}) collective-permute-start(bf16[64,768]{1,0:T(8,128)(2,1)} %bitcast.2), channel_id=1, source_target_pairs={{0,2},{1,3},{2,4},{3,5},{4,6},{5,7},{6,8},{7,9},{8,10},{9,11},{10,... | collective-permute-start | bytes 294920 | tf_op jit(solution)/shard_map/prev/ppermute | solution.py:114
  2.6 4.0 %collective-permute-start = (bf16[64,768]{1,0:T(8,128)(2,1)}, bf16[64,768]{1,0:T(8,128)(2,1)S(1)}, u32[]{:S(2)}, u32[]{:S(2)}) collective-permute-start(bf16[64,768]{1,0:T(8,128)(2,1)} %bitcast.3), channel_id=1, source_target_pairs={{0,14},{1,15},{2,0},{3,1},{4,2},{5,3},{6,4},{7,5},{8,6},{9,7},{10,... | collective-permute-start | bytes 294920 | tf_op jit(solution)/shard_map/next/ppermute | solution.py:114
  6.7 1.2 %collective-permute-start.5 = (bf16[64,1024]{1,0:T(8,128)(2,1)}, bf16[64,1024]{1,0:T(8,128)(2,1)S(1)}, u32[]{:S(2)}, u32[]{:S(2)}) collective-permute-start(bf16[64,1024]{1,0:T(8,128)(2,1)} %refs_0_.1), channel_id=1, source_target_pairs={{0,128},{1,129},{2,130},{3,131},{4,132},{5,133},{6,134},{7,135},{8... | collective-permute-start | bytes 393224 | tf_op jit(solution)/shard_map/half/ppermute | solution.py:114
  7.9 4.5 %collective-permute-start.2 = (bf16[64,768]{1,0:T(8,128)(2,1)}, bf16[64,768]{1,0:T(8,128)(2,1)S(1)}, u32[]{:S(2)}, u32[]{:S(2)}) collective-permute-start(bf16[64,768]{1,0:T(8,128)(2,1)} %bitcast.4), channel_id=1, source_target_pairs={{0,8},{1,9},{2,10},{3,11},{4,12},{5,13},{6,14},{7,15},{8,0},{9,1},... | collective-permute-start | bytes 294920 | tf_op jit(solution)/shard_map/far/ppermute | solution.py:114
  12.4 0.1 collective-permute-start.11
  12.5 0.8 %collective-permute-done.5.refs_1_ = bf16[64,1024]{1,0:T(8,128)(2,1)S(1)} collective-permute-done((bf16[64,1024]{1,0:T(8,128)(2,1)}, bf16[64,1024]{1,0:T(8,128)(2,1)S(1)}, u32[]{:S(2)}, u32[]{:S(2)}) %collective-permute-start.5) | collective-permute-done | bytes 131104 | tf_op jit(solution)/shard_map/half/ppermute | solution.py:114
  13.4 0.6 %collective-permute-start.8 = (bf16[128,1024]{1,0:T(8,128)(2,1)S(1)}, bf16[128,1024]{1,0:T(8,128)(2,1)S(1)}, u32[]{:S(2)}, u32[]{:S(2)}) collective-permute-start(bf16[128,1024]{1,0:T(8,128)(2,1)S(1)} %shard_map.79.refs_0_), channel_id=1, source_target_pairs={{0,32},{1,33},{2,34},{3,35},{4,36},{5,37},{6,38},{7,39},{8,40},{9,... | collective-permute-start | bytes 786440 | tf_op jit(solution)/shard_map/x3/ppermute | solution.py:114
  13.9 1.5 %collective-permute-start.6 = (bf16[128,1024]{1,0:T(8,128)(2,1)S(1)}, bf16[128,1024]{1,0:T(8,128)(2,1)S(1)}, u32[]{:S(2)}, u32[]{:S(2)}) collective-permute-start(bf16[128,1024]{1,0:T(8,128)(2,1)S(1)} %shard_map.79.refs_0_), channel_id=1, source_target_pairs={{0,96},{1,97},{2,98},{3,99},{4,100},{5,101},{6,102},{7,103},{8,104... | collective-permute-start | bytes 786440 | tf_op jit(solution)/shard_map/x1/ppermute | solution.py:114
  15.5 3.1 %collective-permute-done.2.refs_1_.refs_0_.refs_2_ = bf16[64,768]{1,0:T(8,128)(2,1)S(1)} collective-permute-done((bf16[64,768]{1,0:T(8,128)(2,1)}, bf16[64,768]{1,0:T(8,128)(2,1)S(1)}, u32[]{:S(2)}, u32[]{:S(2)}) %collective-permute-start.2) | collective-permute-done | bytes 98336 | tf_op jit(solution)/shard_map/far/ppermute | solution.py:114
  18.6 1.4 %collective-permute-start.15 = (bf16[128,1024]{1,0:T(8,128)(2,1)S(1)}, bf16[128,1024]{1,0:T(8,128)(2,1)S(1)}, u32[]{:S(2)}, u32[]{:S(2)}) collective-permute-start(bf16[128,1024]{1,0:T(8,128)(2,1)S(1)} %shard_map.79.refs_0_), channel_id=1, source_target_pairs={{0,64},{1,65},{2,66},{3,67},{4,68},{5,69},{6,70},{7,71},{8,72},{9,... | collective-permute-start | bytes 786440 | tf_op jit(solution)/shard_map/x2/ppermute | solution.py:114
  20.0 3.2 %collective-permute-done.12.refs_1_.refs_0_.refs_7_ = bf16[64,768]{1,0:T(8,128)(2,1)S(1)} collective-permute-done((bf16[64,768]{1,0:T(8,128)(2,1)S(1)}, bf16[64,768]{1,0:T(8,128)(2,1)S(1)}, u32[]{:S(2)}, u32[]{:S(2)}) %collective-permute-start.12) | collective-permute-done | bytes 98336 | tf_op jit(solution)/shard_map/low_far/ppermute | solution.py:114
  23.2 0.5 %collective-permute-start.13 = (bf16[128,768]{1,0:T(8,128)(2,1)S(1)}, bf16[128,768]{1,0:T(8,128)(2,1)S(1)}, u32[]{:S(2)}, u32[]{:S(2)}) collective-permute-start(bf16[128,768]{1,0:T(8,128)(2,1)S(1)} %shard_map.80), channel_id=1, source_target_pairs={{0,14},{1,15},{2,0},{3,1},{4,2},{5,3},{6,4},{7,5},{8,6},{9,7},{10,... | collective-permute-start | bytes 589832 | tf_op jit(solution)/shard_map/lup/ppermute | solution.py:114
  23.7 3.4 %collective-permute-done.6.refs_1_ = bf16[128,1024]{1,0:T(8,128)(2,1)S(1)} collective-permute-done((bf16[128,1024]{1,0:T(8,128)(2,1)S(1)}, bf16[128,1024]{1,0:T(8,128)(2,1)S(1)}, u32[]{:S(2)}, u32[]{:S(2)}) %collective-permute-start.6) | collective-permute-done | bytes 262176 | tf_op jit(solution)/shard_map/x1/ppermute | solution.py:114
  27.2 0.1 collective-permute-start.14
  27.3 0.0 copy-start
  27.3 3.3 %collective-permute-start.3 = (bf16[128,768]{1,0:T(8,128)(2,1)S(1)}, bf16[128,768]{1,0:T(8,128)(2,1)S(1)}, u32[]{:S(2)}, u32[]{:S(2)}) collective-permute-start(bf16[128,768]{1,0:T(8,128)(2,1)S(1)} %shard_map.77), channel_id=1, source_target_pairs={{0,14},{1,15},{2,0},{3,1},{4,2},{5,3},{6,4},{7,5},{8,6},{9,7},{10,... | collective-permute-start | bytes 589832 | tf_op jit(solution)/shard_map/up/ppermute | solution.py:114
  30.6 0.1 collective-permute-start.16
  30.7 0.5 %collective-permute-start.17 = (bf16[128,1024]{1,0:T(8,128)(2,1)S(1)}, bf16[128,1024]{1,0:T(8,128)(2,1)S(1)}, u32[]{:S(2)}, u32[]{:S(2)}) collective-permute-start(bf16[128,1024]{1,0:T(8,128)(2,1)S(1)} %collective-permute-done.15.refs_3_), channel_id=1, source_target_pairs={{0,16},{1,17},{2,18},{3,19},{4,20},{5,21},{6,22},{7,23},{8,24},{9,... | collective-permute-start | bytes 786440 | tf_op jit(solution)/shard_map/c3/ppermute | solution.py:114
  31.2 4.9 %collective-permute-done.14.refs_1_ = bf16[128,768]{1,0:T(8,128)(2,1)S(1)} collective-permute-done((bf16[128,768]{1,0:T(8,128)(2,1)S(1)}, bf16[128,768]{1,0:T(8,128)(2,1)S(1)}, u32[]{:S(2)}, u32[]{:S(2)}) %collective-permute-start.14) | collective-permute-done | bytes 196640 | tf_op jit(solution)/shard_map/ldn/ppermute | solution.py:114
  36.2 0.0 copy-start.1
  36.2 2.3 %shard_map.83 = (bf16[1024,1024]{1,0:T(8,128)(2,1)S(1)}, bf16[64,1024]{1,0:T(8,128)(2,1)}) custom-call(bf16[128,1024]{1,0:T(8,128)(2,1)S(1)} %shard_map.79.refs_0_, bf16[128,1024]{1,0:T(8,128)(2,1)S(1)} %collective-permute-done.6.refs_1_, bf16[128,1024]{1,0:T(8,128)(2,1)S(1)} %collective-permute-done.8.refs_2_, ...), custom_call_target="tpu_custom_call" | custom-call | tf_op jit(solution)/shard_map/pallas_call | solution.py:186
  38.6 1.4 %collective-permute-done.4.refs_4_ = bf16[128,768]{1,0:T(8,128)(2,1)S(1)} collective-permute-done((bf16[128,768]{1,0:T(8,128)(2,1)S(1)}, bf16[128,768]{1,0:T(8,128)(2,1)S(1)}, u32[]{:S(2)}, u32[]{:S(2)}) %collective-permute-start.4) | collective-permute-done | bytes 196640 | tf_op jit(solution)/shard_map/down/ppermute | solution.py:114
  40.0 0.8 %collective-permute-done.10.refs_5_ = bf16[64,768]{1,0:T(8,128)(2,1)S(1)} collective-permute-done((bf16[64,768]{1,0:T(8,128)(2,1)S(1)}, bf16[64,768]{1,0:T(8,128)(2,1)S(1)}, u32[]{:S(2)}, u32[]{:S(2)}) %collective-permute-start.10) | collective-permute-done | bytes 98336 | tf_op jit(solution)/shard_map/low_own/ppermute | solution.py:114
  40.8 4.3 %shard_map.84 = (bf16[64,768]{1,0:T(8,128)(2,1)}, f32[768,1024]{1,0:T(8,128)}) custom-call(bf16[64,768]{1,0:T(8,128)(2,1)S(1)} %bitcast.6, bf16[128,768]{1,0:T(8,128)(2,1)S(1)} %shard_map.76.refs_1_, bf16[64,768]{1,0:T(8,128)(2,1)S(1)} %collective-permute-done.2.refs_1_.refs_0_.refs_2_, bf16[128,768]{1,0:T(8,128)(2,1)S(1)} %collective-permute-done.3.refs_3_, ...), custom_call_target="tpu_custom_call" | custom-call | flops 3221225472 | tf_op jit(solution)/shard_map/pallas_call | solution.py:199
  (31 shorter events, 0.2 us)
Async XLA Ops:
  0.6 12.7 %copy-start.3 = (bf16[64,1024]{1,0:T(8,128)(2,1)S(1)}, bf16[64,1024]{1,0:T(8,128)(2,1)}, u32[]{:S(2)}) copy-start(bf16[64,1024]{1,0:T(8,128)(2,1)} %refs_0_.1) | copy-start | bytes 393220
  0.6 11.7 %collective-permute-start.1 = (bf16[64,768]{1,0:T(8,128)(2,1)}, bf16[64,768]{1,0:T(8,128)(2,1)S(1)}, u32[]{:S(2)}, u32[]{:S(2)}) collective-permute-start(bf16[64,768]{1,0:T(8,128)(2,1)} %bitcast.2), channel_id=1, source_target_pairs={{0,2},{1,3},{2,4},{3,5},{4,6},{5,7},{6,8},{7,9},{8,10},{9,11},{10,... | collective-permute-start | bytes 294920 | tf_op jit(solution)/shard_map/prev/ppermute | solution.py:114
  2.6 9.8 %collective-permute-start = (bf16[64,768]{1,0:T(8,128)(2,1)}, bf16[64,768]{1,0:T(8,128)(2,1)S(1)}, u32[]{:S(2)}, u32[]{:S(2)}) collective-permute-start(bf16[64,768]{1,0:T(8,128)(2,1)} %bitcast.3), channel_id=1, source_target_pairs={{0,14},{1,15},{2,0},{3,1},{4,2},{5,3},{6,4},{7,5},{8,6},{9,7},{10,... | collective-permute-start | bytes 294920 | tf_op jit(solution)/shard_map/next/ppermute | solution.py:114
  6.7 6.7 %collective-permute-start.5 = (bf16[64,1024]{1,0:T(8,128)(2,1)}, bf16[64,1024]{1,0:T(8,128)(2,1)S(1)}, u32[]{:S(2)}, u32[]{:S(2)}) collective-permute-start(bf16[64,1024]{1,0:T(8,128)(2,1)} %refs_0_.1), channel_id=1, source_target_pairs={{0,128},{1,129},{2,130},{3,131},{4,132},{5,133},{6,134},{7,135},{8... | collective-permute-start | bytes 393224 | tf_op jit(solution)/shard_map/half/ppermute | solution.py:114
  7.9 10.7 %collective-permute-start.2 = (bf16[64,768]{1,0:T(8,128)(2,1)}, bf16[64,768]{1,0:T(8,128)(2,1)S(1)}, u32[]{:S(2)}, u32[]{:S(2)}) collective-permute-start(bf16[64,768]{1,0:T(8,128)(2,1)} %bitcast.4), channel_id=1, source_target_pairs={{0,8},{1,9},{2,10},{3,11},{4,12},{5,13},{6,14},{7,15},{8,0},{9,1},... | collective-permute-start | bytes 294920 | tf_op jit(solution)/shard_map/far/ppermute | solution.py:114
  12.4 10.8 %collective-permute-start.11 = (bf16[128,768]{1,0:T(8,128)(2,1)S(1)}, bf16[128,768]{1,0:T(8,128)(2,1)S(1)}, u32[]{:S(2)}, u32[]{:S(2)}) collective-permute-start(bf16[128,768]{1,0:T(8,128)(2,1)S(1)} %shard_map.76.refs_1_), channel_id=1, source_target_pairs={{0,1},{1,0},{2,3},{3,2},{4,5},{5,4},{6,7},{7,6},{8,9},{9,8},{10,11... | collective-permute-start | bytes 589832 | tf_op jit(solution)/shard_map/low_pair/ppermute | solution.py:114
  13.4 10.4 %collective-permute-start.8 = (bf16[128,1024]{1,0:T(8,128)(2,1)S(1)}, bf16[128,1024]{1,0:T(8,128)(2,1)S(1)}, u32[]{:S(2)}, u32[]{:S(2)}) collective-permute-start(bf16[128,1024]{1,0:T(8,128)(2,1)S(1)} %shard_map.79.refs_0_), channel_id=1, source_target_pairs={{0,32},{1,33},{2,34},{3,35},{4,36},{5,37},{6,38},{7,39},{8,40},{9,... | collective-permute-start | bytes 786440 | tf_op jit(solution)/shard_map/x3/ppermute | solution.py:114
  13.9 13.2 %collective-permute-start.6 = (bf16[128,1024]{1,0:T(8,128)(2,1)S(1)}, bf16[128,1024]{1,0:T(8,128)(2,1)S(1)}, u32[]{:S(2)}, u32[]{:S(2)}) collective-permute-start(bf16[128,1024]{1,0:T(8,128)(2,1)S(1)} %shard_map.79.refs_0_), channel_id=1, source_target_pairs={{0,96},{1,97},{2,98},{3,99},{4,100},{5,101},{6,102},{7,103},{8,104... | collective-permute-start | bytes 786440 | tf_op jit(solution)/shard_map/x1/ppermute | solution.py:114
  18.6 4.6 %collective-permute-start.12 = (bf16[64,768]{1,0:T(8,128)(2,1)S(1)}, bf16[64,768]{1,0:T(8,128)(2,1)S(1)}, u32[]{:S(2)}, u32[]{:S(2)}) collective-permute-start(bf16[64,768]{1,0:T(8,128)(2,1)S(1)} %collective-permute-done.2.refs_1_.refs_0_.refs_2_), channel_id=1, source_target_pairs={{0,1},{1,0},{2,3},{3,2},{4,5},{5,4},{6,7},{7,6},{8,9},{9,8},{10,11... | collective-permute-start | bytes 294920 | tf_op jit(solution)/shard_map/low_far/ppermute | solution.py:114
  18.6 12.0 %collective-permute-start.15 = (bf16[128,1024]{1,0:T(8,128)(2,1)S(1)}, bf16[128,1024]{1,0:T(8,128)(2,1)S(1)}, u32[]{:S(2)}, u32[]{:S(2)}) collective-permute-start(bf16[128,1024]{1,0:T(8,128)(2,1)S(1)} %shard_map.79.refs_0_), channel_id=1, source_target_pairs={{0,64},{1,65},{2,66},{3,67},{4,68},{5,69},{6,70},{7,71},{8,72},{9,... | collective-permute-start | bytes 786440 | tf_op jit(solution)/shard_map/x2/ppermute | solution.py:114
  23.2 12.9 %copy-start.4 = (bf16[768,64]{0,1:T(8,128)(2,1)S(1)}, bf16[768,64]{0,1:T(8,128)(2,1)}, u32[]{:S(2)}) copy-start(bf16[768,64]{0,1:T(8,128)(2,1)} %param.6) | copy-start | bytes 294916
  23.2 7.5 %collective-permute-start.13 = (bf16[128,768]{1,0:T(8,128)(2,1)S(1)}, bf16[128,768]{1,0:T(8,128)(2,1)S(1)}, u32[]{:S(2)}, u32[]{:S(2)}) collective-permute-start(bf16[128,768]{1,0:T(8,128)(2,1)S(1)} %shard_map.80), channel_id=1, source_target_pairs={{0,14},{1,15},{2,0},{3,1},{4,2},{5,3},{6,4},{7,5},{8,6},{9,7},{10,... | collective-permute-start | bytes 589832 | tf_op jit(solution)/shard_map/lup/ppermute | solution.py:114
  23.7 3.6 %collective-permute-start.9 = (bf16[128,1024]{1,0:T(8,128)(2,1)S(1)}, bf16[128,1024]{1,0:T(8,128)(2,1)S(1)}, u32[]{:S(2)}, u32[]{:S(2)}) collective-permute-start(bf16[128,1024]{1,0:T(8,128)(2,1)S(1)} %collective-permute-done.8.refs_2_), channel_id=1, source_target_pairs={{0,16},{1,17},{2,18},{3,19},{4,20},{5,21},{6,22},{7,23},{8,24},{9,... | collective-permute-start | bytes 786440 | tf_op jit(solution)/shard_map/c2/ppermute | solution.py:114
  27.1 3.5 %collective-permute-start.7 = (bf16[128,1024]{1,0:T(8,128)(2,1)S(1)}, bf16[128,1024]{1,0:T(8,128)(2,1)S(1)}, u32[]{:S(2)}, u32[]{:S(2)}) collective-permute-start(bf16[128,1024]{1,0:T(8,128)(2,1)S(1)} %collective-permute-done.6.refs_1_), channel_id=1, source_target_pairs={{0,16},{1,17},{2,18},{3,19},{4,20},{5,21},{6,22},{7,23},{8,24},{9,... | collective-permute-start | bytes 786440 | tf_op jit(solution)/shard_map/c1/ppermute | solution.py:114
  27.2 9.0 %collective-permute-start.14 = (bf16[128,768]{1,0:T(8,128)(2,1)S(1)}, bf16[128,768]{1,0:T(8,128)(2,1)S(1)}, u32[]{:S(2)}, u32[]{:S(2)}) collective-permute-start(bf16[128,768]{1,0:T(8,128)(2,1)S(1)} %shard_map.81), channel_id=1, source_target_pairs={{0,2},{1,3},{2,4},{3,5},{4,6},{5,7},{6,8},{7,9},{8,10},{9,11},{10,... | collective-permute-start | bytes 589832 | tf_op jit(solution)/shard_map/ldn/ppermute | solution.py:114
  27.3 8.9 %copy-start = (bf16[1024,1024]{1,0:T(8,128)(2,1)S(1)}, bf16[1024,1024]{1,0:T(8,128)(2,1)}, u32[]{:S(2)}) copy-start(bf16[1024,1024]{1,0:T(8,128)(2,1)} %refs_8_.1) | copy-start | bytes 6291460
  27.3 11.3 %collective-permute-start.3 = (bf16[128,768]{1,0:T(8,128)(2,1)S(1)}, bf16[128,768]{1,0:T(8,128)(2,1)S(1)}, u32[]{:S(2)}, u32[]{:S(2)}) collective-permute-start(bf16[128,768]{1,0:T(8,128)(2,1)S(1)} %shard_map.77), channel_id=1, source_target_pairs={{0,14},{1,15},{2,0},{3,1},{4,2},{5,3},{6,4},{7,5},{8,6},{9,7},{10,... | collective-permute-start | bytes 589832 | tf_op jit(solution)/shard_map/up/ppermute | solution.py:114
  30.6 9.4 %collective-permute-start.4 = (bf16[128,768]{1,0:T(8,128)(2,1)S(1)}, bf16[128,768]{1,0:T(8,128)(2,1)S(1)}, u32[]{:S(2)}, u32[]{:S(2)}) collective-permute-start(bf16[128,768]{1,0:T(8,128)(2,1)S(1)} %shard_map.78), channel_id=1, source_target_pairs={{0,2},{1,3},{2,4},{3,5},{4,6},{5,7},{6,8},{7,9},{8,10},{9,11},{10,... | collective-permute-start | bytes 589832 | tf_op jit(solution)/shard_map/down/ppermute | solution.py:114
  30.6 5.6 %collective-permute-start.16 = (bf16[128,1024]{1,0:T(8,128)(2,1)S(1)}, bf16[128,1024]{1,0:T(8,128)(2,1)S(1)}, u32[]{:S(2)}, u32[]{:S(2)}) collective-permute-start(bf16[128,1024]{1,0:T(8,128)(2,1)S(1)} %shard_map.79.refs_0_), channel_id=1, source_target_pairs={{0,16},{1,17},{2,18},{3,19},{4,20},{5,21},{6,22},{7,23},{8,24},{9,... | collective-permute-start | bytes 786440 | tf_op jit(solution)/shard_map/c0/ppermute | solution.py:114
  30.7 5.5 %collective-permute-start.17 = (bf16[128,1024]{1,0:T(8,128)(2,1)S(1)}, bf16[128,1024]{1,0:T(8,128)(2,1)S(1)}, u32[]{:S(2)}, u32[]{:S(2)}) collective-permute-start(bf16[128,1024]{1,0:T(8,128)(2,1)S(1)} %collective-permute-done.15.refs_3_), channel_id=1, source_target_pairs={{0,16},{1,17},{2,18},{3,19},{4,20},{5,21},{6,22},{7,23},{8,24},{9,... | collective-permute-start | bytes 786440 | tf_op jit(solution)/shard_map/c3/ppermute | solution.py:114
  36.1 4.6 %collective-permute-start.10 = (bf16[64,768]{1,0:T(8,128)(2,1)S(1)}, bf16[64,768]{1,0:T(8,128)(2,1)S(1)}, u32[]{:S(2)}, u32[]{:S(2)}) collective-permute-start(bf16[64,768]{1,0:T(8,128)(2,1)S(1)} %bitcast.5), channel_id=1, source_target_pairs={{0,1},{1,0},{2,3},{3,2},{4,5},{5,4},{6,7},{7,6},{8,9},{9,8},{10,11... | collective-permute-start | bytes 294920 | tf_op jit(solution)/shard_map/low_own/ppermute | solution.py:114
  36.1 4.6 %copy-start.2 = (bf16[1024,1024]{1,0:T(8,128)(2,1)S(1)}, bf16[1024,1024]{1,0:T(8,128)(2,1)}, u32[]{:S(2)}) copy-start(bf16[1024,1024]{1,0:T(8,128)(2,1)} %refs_9_.1) | copy-start | bytes 6291460
  36.2 4.6 %copy-start.1 = (f32[768,1024]{1,0:T(8,128)S(1)}, f32[768,1024]{1,0:T(8,128)}, u32[]{:S(2)}) copy-start(f32[768,1024]{1,0:T(8,128)} %refs_11_.1) | copy-start | bytes 9437188

commit v5 on v4

--- a/solution.py
+++ b/solution.py
@@ -155,7 +155,6 @@
     low_pair = from_low(pair, "low_pair")
     b_x1 = from_x(b_two, "x1", 1)
     b_x3 = from_x(b_two, "x3", 3)
-    b_c0 = from_core(b_two, "c0")
     b_x2 = from_x(b_two, "x2", 2)
     low_far = from_low(a_far, "low_far")
     for_up = join(0, a_next, a_far)
@@ -164,6 +163,7 @@
     down = from_z(for_down, "down", -1)
     b_c1 = from_core(b_x1, "c1")
     b_c2 = from_core(b_x3, "c2")
+    b_c0 = from_core(after(b_two, b_c1, b_c2), "c0")
     low_own = from_low(after(own_a, b_c1, b_c2), "low_own")
     for_low_up = join(1, (low_pair, 0, share), low_far)
     for_low_down = join(1, low_far, (low_pair, share, share))

time: 45.3 us -> 44.9 us (level)
  the two profiles are of different devices: /device:TPU:30 before, /device:TPU:1 now
where the time goes in v5:
time: 44.9 us; the launch traced here: 44.6 us
  starting transfers between devices  33.8 us (75%)
  Pallas kernels  6.73 us (15%)
  waiting for transfers between devices  3.08 us (7%)
  between operations  0.94 us (2%)
    ppermute x18, starting transfers between devices, send(): return lax.ppermute(block, ('row', 'col'), pairs_of(16, 16, target))  33.8 us
    pallas_call x1, Pallas kernels, on_device(): pl.pallas_call(functools.partial(update_kernel, a_places), out_shape=[jax...  4.28 us
    ppermute x18, waiting for transfers between devices, send(): return lax.ppermute(block, ('row', 'col'), pairs_of(16, 16, target))  3.08 us
    pallas_call x1, Pallas kernels, on_device(): pl.pallas_call(functools.partial(upper_kernel, b_places), out_shape=[jax....  2.34 us
  transfers between devices with their start and end apart: 18, of which 4 were waited for; matrix products, arithmetic and copies ran while one was open for 0% of the time, Pallas kernels for 5%

profile of v5, /device:TPU:1, one launch (start us, length us, event | category | flops | bytes accessed | tf_op | source)
XLA Modules:
  0.0 44.6 jit_solution(14362048217519772917)
XLA Ops:
  0.6 2.5 %collective-permute-start.1 = (bf16[64,768]{1,0:T(8,128)(2,1)}, bf16[64,768]{1,0:T(8,128)(2,1)S(1)}, u32[]{:S(2)}, u32[]{:S(2)}) collective-permute-start(bf16[64,768]{1,0:T(8,128)(2,1)} %bitcast.2), channel_id=1, source_target_pairs={{0,2},{1,3},{2,4},{3,5},{4,6},{5,7},{6,8},{7,9},{8,10},{9,11},{10,... | collective-permute-start | bytes 294920 | tf_op jit(solution)/shard_map/prev/ppermute | solution.py:114
  3.2 4.0 %collective-permute-start = (bf16[64,768]{1,0:T(8,128)(2,1)}, bf16[64,768]{1,0:T(8,128)(2,1)S(1)}, u32[]{:S(2)}, u32[]{:S(2)}) collective-permute-start(bf16[64,768]{1,0:T(8,128)(2,1)} %bitcast.3), channel_id=1, source_target_pairs={{0,14},{1,15},{2,0},{3,1},{4,2},{5,3},{6,4},{7,5},{8,6},{9,7},{10,... | collective-permute-start | bytes 294920 | tf_op jit(solution)/shard_map/next/ppermute | solution.py:114
  7.2 2.9 %collective-permute-start.5 = (bf16[64,1024]{1,0:T(8,128)(2,1)}, bf16[64,1024]{1,0:T(8,128)(2,1)S(1)}, u32[]{:S(2)}, u32[]{:S(2)}) collective-permute-start(bf16[64,1024]{1,0:T(8,128)(2,1)} %refs_0_.1), channel_id=1, source_target_pairs={{0,128},{1,129},{2,130},{3,131},{4,132},{5,133},{6,134},{7,135},{8... | collective-permute-start | bytes 393224 | tf_op jit(solution)/shard_map/half/ppermute | solution.py:114
  10.1 3.9 %collective-permute-start.2 = (bf16[64,768]{1,0:T(8,128)(2,1)}, bf16[64,768]{1,0:T(8,128)(2,1)S(1)}, u32[]{:S(2)}, u32[]{:S(2)}) collective-permute-start(bf16[64,768]{1,0:T(8,128)(2,1)} %bitcast.4), channel_id=1, source_target_pairs={{0,8},{1,9},{2,10},{3,11},{4,12},{5,13},{6,14},{7,15},{8,0},{9,1},... | collective-permute-start | bytes 294920 | tf_op jit(solution)/shard_map/far/ppermute | solution.py:114
  14.1 0.5 %collective-permute-start.11 = (bf16[128,768]{1,0:T(8,128)(2,1)S(1)}, bf16[128,768]{1,0:T(8,128)(2,1)S(1)}, u32[]{:S(2)}, u32[]{:S(2)}) collective-permute-start(bf16[128,768]{1,0:T(8,128)(2,1)S(1)} %shard_map.76.refs_1_), channel_id=1, source_target_pairs={{0,1},{1,0},{2,3},{3,2},{4,5},{5,4},{6,7},{7,6},{8,9},{9,8},{10,11... | collective-permute-start | bytes 589832 | tf_op jit(solution)/shard_map/low_pair/ppermute | solution.py:114
  14.6 1.3 %collective-permute-start.8 = (bf16[128,1024]{1,0:T(8,128)(2,1)S(1)}, bf16[128,1024]{1,0:T(8,128)(2,1)S(1)}, u32[]{:S(2)}, u32[]{:S(2)}) collective-permute-start(bf16[128,1024]{1,0:T(8,128)(2,1)S(1)} %shard_map.79.refs_0_), channel_id=1, source_target_pairs={{0,32},{1,33},{2,34},{3,35},{4,36},{5,37},{6,38},{7,39},{8,40},{9,... | collective-permute-start | bytes 786440 | tf_op jit(solution)/shard_map/x3/ppermute | solution.py:114
  15.9 1.5 %collective-permute-start.6 = (bf16[128,1024]{1,0:T(8,128)(2,1)S(1)}, bf16[128,1024]{1,0:T(8,128)(2,1)S(1)}, u32[]{:S(2)}, u32[]{:S(2)}) collective-permute-start(bf16[128,1024]{1,0:T(8,128)(2,1)S(1)} %shard_map.79.refs_0_), channel_id=1, source_target_pairs={{0,96},{1,97},{2,98},{3,99},{4,100},{5,101},{6,102},{7,103},{8,104... | collective-permute-start | bytes 786440 | tf_op jit(solution)/shard_map/x1/ppermute | solution.py:114
  17.3 0.4 collective-permute-done.2.refs_1_.refs_0_.refs_2_
  17.7 0.7 %collective-permute-start.12 = (bf16[64,768]{1,0:T(8,128)(2,1)S(1)}, bf16[64,768]{1,0:T(8,128)(2,1)S(1)}, u32[]{:S(2)}, u32[]{:S(2)}) collective-permute-start(bf16[64,768]{1,0:T(8,128)(2,1)S(1)} %collective-permute-done.2.refs_1_.refs_0_.refs_2_), channel_id=1, source_target_pairs={{0,1},{1,0},{2,3},{3,2},{4,5},{5,4},{6,7},{7,6},{8,9},{9,8},{10,11... | collective-permute-start | bytes 294920 | tf_op jit(solution)/shard_map/low_far/ppermute | solution.py:114
  18.4 2.4 %collective-permute-start.15 = (bf16[128,1024]{1,0:T(8,128)(2,1)S(1)}, bf16[128,1024]{1,0:T(8,128)(2,1)S(1)}, u32[]{:S(2)}, u32[]{:S(2)}) collective-permute-start(bf16[128,1024]{1,0:T(8,128)(2,1)S(1)} %shard_map.79.refs_0_), channel_id=1, source_target_pairs={{0,64},{1,65},{2,66},{3,67},{4,68},{5,69},{6,70},{7,71},{8,72},{9,... | collective-permute-start | bytes 786440 | tf_op jit(solution)/shard_map/x2/ppermute | solution.py:114
  20.9 1.4 %collective-permute-done.12.refs_1_.refs_0_.refs_7_ = bf16[64,768]{1,0:T(8,128)(2,1)S(1)} collective-permute-done((bf16[64,768]{1,0:T(8,128)(2,1)S(1)}, bf16[64,768]{1,0:T(8,128)(2,1)S(1)}, u32[]{:S(2)}, u32[]{:S(2)}) %collective-permute-start.12) | collective-permute-done | bytes 98336 | tf_op jit(solution)/shard_map/low_far/ppermute | solution.py:114
  22.3 2.3 %collective-permute-start.13 = (bf16[128,768]{1,0:T(8,128)(2,1)S(1)}, bf16[128,768]{1,0:T(8,128)(2,1)S(1)}, u32[]{:S(2)}, u32[]{:S(2)}) collective-permute-start(bf16[128,768]{1,0:T(8,128)(2,1)S(1)} %shard_map.80), channel_id=1, source_target_pairs={{0,14},{1,15},{2,0},{3,1},{4,2},{5,3},{6,4},{7,5},{8,6},{9,7},{10,... | collective-permute-start | bytes 589832 | tf_op jit(solution)/shard_map/lup/ppermute | solution.py:114
  24.6 2.4 %collective-permute-start.9 = (bf16[128,1024]{1,0:T(8,128)(2,1)S(1)}, bf16[128,1024]{1,0:T(8,128)(2,1)S(1)}, u32[]{:S(2)}, u32[]{:S(2)}) collective-permute-start(bf16[128,1024]{1,0:T(8,128)(2,1)S(1)} %collective-permute-done.8.refs_2_), channel_id=1, source_target_pairs={{0,16},{1,17},{2,18},{3,19},{4,20},{5,21},{6,22},{7,23},{8,24},{9,... | collective-permute-start | bytes 786440 | tf_op jit(solution)/shard_map/c2/ppermute | solution.py:114
  27.0 0.1 collective-permute-start.7
  27.1 1.6 %collective-permute-start.14 = (bf16[128,768]{1,0:T(8,128)(2,1)S(1)}, bf16[128,768]{1,0:T(8,128)(2,1)S(1)}, u32[]{:S(2)}, u32[]{:S(2)}) collective-permute-start(bf16[128,768]{1,0:T(8,128)(2,1)S(1)} %shard_map.81), channel_id=1, source_target_pairs={{0,2},{1,3},{2,4},{3,5},{4,6},{5,7},{6,8},{7,9},{8,10},{9,11},{10,... | collective-permute-start | bytes 589832 | tf_op jit(solution)/shard_map/ldn/ppermute | solution.py:114
  28.8 1.2 %collective-permute-start.3 = (bf16[128,768]{1,0:T(8,128)(2,1)S(1)}, bf16[128,768]{1,0:T(8,128)(2,1)S(1)}, u32[]{:S(2)}, u32[]{:S(2)}) collective-permute-start(bf16[128,768]{1,0:T(8,128)(2,1)S(1)} %shard_map.77), channel_id=1, source_target_pairs={{0,14},{1,15},{2,0},{3,1},{4,2},{5,3},{6,4},{7,5},{8,6},{9,7},{10,... | collective-permute-start | bytes 589832 | tf_op jit(solution)/shard_map/up/ppermute | solution.py:114
  30.0 0.3 collective-permute-start.4
  30.3 2.9 %collective-permute-start.17 = (bf16[128,1024]{1,0:T(8,128)(2,1)S(1)}, bf16[128,1024]{1,0:T(8,128)(2,1)S(1)}, u32[]{:S(2)}, u32[]{:S(2)}) collective-permute-start(bf16[128,1024]{1,0:T(8,128)(2,1)S(1)} %collective-permute-done.15.refs_3_), channel_id=1, source_target_pairs={{0,16},{1,17},{2,18},{3,19},{4,20},{5,21},{6,22},{7,23},{8,24},{9,... | collective-permute-start | bytes 786440 | tf_op jit(solution)/shard_map/c3/ppermute | solution.py:114
  33.2 1.1 %collective-permute-start.10 = (bf16[64,768]{1,0:T(8,128)(2,1)S(1)}, bf16[64,768]{1,0:T(8,128)(2,1)S(1)}, u32[]{:S(2)}, u32[]{:S(2)}) collective-permute-start(bf16[64,768]{1,0:T(8,128)(2,1)S(1)} %bitcast.5), channel_id=1, source_target_pairs={{0,1},{1,0},{2,3},{3,2},{4,5},{5,4},{6,7},{7,6},{8,9},{9,8},{10,11... | collective-permute-start | bytes 294920 | tf_op jit(solution)/shard_map/low_own/ppermute | solution.py:114
  34.3 0.1 collective-permute-done.14.refs_1_
  34.5 2.1 %collective-permute-start.16 = (bf16[128,1024]{1,0:T(8,128)(2,1)S(1)}, bf16[128,1024]{1,0:T(8,128)(2,1)S(1)}, u32[]{:S(2)}, u32[]{:S(2)}) collective-permute-start(bf16[128,1024]{1,0:T(8,128)(2,1)S(1)} %shard_map.79.refs_0_), channel_id=1, source_target_pairs={{0,16},{1,17},{2,18},{3,19},{4,20},{5,21},{6,22},{7,23},{8,24},{9,... | collective-permute-start | bytes 786440 | tf_op jit(solution)/shard_map/c0/ppermute | solution.py:114
  36.6 1.1 %collective-permute-done.16.refs_4_ = bf16[128,1024]{1,0:T(8,128)(2,1)S(1)} collective-permute-done((bf16[128,1024]{1,0:T(8,128)(2,1)S(1)}, bf16[128,1024]{1,0:T(8,128)(2,1)S(1)}, u32[]{:S(2)}, u32[]{:S(2)}) %collective-permute-start.16) | collective-permute-done | bytes 262176 | tf_op jit(solution)/shard_map/c0/ppermute | solution.py:114
  37.7 2.3 %shard_map.83 = (bf16[1024,1024]{1,0:T(8,128)(2,1)S(1)}, bf16[64,1024]{1,0:T(8,128)(2,1)}) custom-call(bf16[128,1024]{1,0:T(8,128)(2,1)S(1)} %shard_map.79.refs_0_, bf16[128,1024]{1,0:T(8,128)(2,1)S(1)} %collective-permute-done.6.refs_1_, bf16[128,1024]{1,0:T(8,128)(2,1)S(1)} %collective-permute-done.8.refs_2_, ...), custom_call_target="tpu_custom_call" | custom-call | tf_op jit(solution)/shard_map/pallas_call | solution.py:186
  40.1 4.3 %shard_map.84 = (bf16[64,768]{1,0:T(8,128)(2,1)}, f32[768,1024]{1,0:T(8,128)}) custom-call(bf16[64,768]{1,0:T(8,128)(2,1)S(1)} %bitcast.6, bf16[128,768]{1,0:T(8,128)(2,1)S(1)} %shard_map.76.refs_1_, bf16[64,768]{1,0:T(8,128)(2,1)S(1)} %collective-permute-done.2.refs_1_.refs_0_.refs_2_, bf16[128,768]{1,0:T(8,128)(2,1)S(1)} %collective-permute-done.3.refs_3_, ...), custom_call_target="tpu_custom_call" | custom-call | flops 3221225472 | tf_op jit(solution)/shard_map/pallas_call | solution.py:199
  (31 shorter events, 0.2 us)
Async XLA Ops:
  0.6 13.9 %copy-start.3 = (bf16[64,1024]{1,0:T(8,128)(2,1)S(1)}, bf16[64,1024]{1,0:T(8,128)(2,1)}, u32[]{:S(2)}) copy-start(bf16[64,1024]{1,0:T(8,128)(2,1)} %refs_0_.1) | copy-start | bytes 393220
  0.6 13.4 %collective-permute-start.1 = (bf16[64,768]{1,0:T(8,128)(2,1)}, bf16[64,768]{1,0:T(8,128)(2,1)S(1)}, u32[]{:S(2)}, u32[]{:S(2)}) collective-permute-start(bf16[64,768]{1,0:T(8,128)(2,1)} %bitcast.2), channel_id=1, source_target_pairs={{0,2},{1,3},{2,4},{3,5},{4,6},{5,7},{6,8},{7,9},{8,10},{9,11},{10,... | collective-permute-start | bytes 294920 | tf_op jit(solution)/shard_map/prev/ppermute | solution.py:114
  3.2 10.9 %collective-permute-start = (bf16[64,768]{1,0:T(8,128)(2,1)}, bf16[64,768]{1,0:T(8,128)(2,1)S(1)}, u32[]{:S(2)}, u32[]{:S(2)}) collective-permute-start(bf16[64,768]{1,0:T(8,128)(2,1)} %bitcast.3), channel_id=1, source_target_pairs={{0,14},{1,15},{2,0},{3,1},{4,2},{5,3},{6,4},{7,5},{8,6},{9,7},{10,... | collective-permute-start | bytes 294920 | tf_op jit(solution)/shard_map/next/ppermute | solution.py:114
  7.2 7.3 %collective-permute-start.5 = (bf16[64,1024]{1,0:T(8,128)(2,1)}, bf16[64,1024]{1,0:T(8,128)(2,1)S(1)}, u32[]{:S(2)}, u32[]{:S(2)}) collective-permute-start(bf16[64,1024]{1,0:T(8,128)(2,1)} %refs_0_.1), channel_id=1, source_target_pairs={{0,128},{1,129},{2,130},{3,131},{4,132},{5,133},{6,134},{7,135},{8... | collective-permute-start | bytes 393224 | tf_op jit(solution)/shard_map/half/ppermute | solution.py:114
  10.1 7.6 %collective-permute-start.2 = (bf16[64,768]{1,0:T(8,128)(2,1)}, bf16[64,768]{1,0:T(8,128)(2,1)S(1)}, u32[]{:S(2)}, u32[]{:S(2)}) collective-permute-start(bf16[64,768]{1,0:T(8,128)(2,1)} %bitcast.4), channel_id=1, source_target_pairs={{0,8},{1,9},{2,10},{3,11},{4,12},{5,13},{6,14},{7,15},{8,0},{9,1},... | collective-permute-start | bytes 294920 | tf_op jit(solution)/shard_map/far/ppermute | solution.py:114
  14.1 8.2 %collective-permute-start.11 = (bf16[128,768]{1,0:T(8,128)(2,1)S(1)}, bf16[128,768]{1,0:T(8,128)(2,1)S(1)}, u32[]{:S(2)}, u32[]{:S(2)}) collective-permute-start(bf16[128,768]{1,0:T(8,128)(2,1)S(1)} %shard_map.76.refs_1_), channel_id=1, source_target_pairs={{0,1},{1,0},{2,3},{3,2},{4,5},{5,4},{6,7},{7,6},{8,9},{9,8},{10,11... | collective-permute-start | bytes 589832 | tf_op jit(solution)/shard_map/low_pair/ppermute | solution.py:114
  14.6 10.0 %collective-permute-start.8 = (bf16[128,1024]{1,0:T(8,128)(2,1)S(1)}, bf16[128,1024]{1,0:T(8,128)(2,1)S(1)}, u32[]{:S(2)}, u32[]{:S(2)}) collective-permute-start(bf16[128,1024]{1,0:T(8,128)(2,1)S(1)} %shard_map.79.refs_0_), channel_id=1, source_target_pairs={{0,32},{1,33},{2,34},{3,35},{4,36},{5,37},{6,38},{7,39},{8,40},{9,... | collective-permute-start | bytes 786440 | tf_op jit(solution)/shard_map/x3/ppermute | solution.py:114
  15.9 11.1 %collective-permute-start.6 = (bf16[128,1024]{1,0:T(8,128)(2,1)S(1)}, bf16[128,1024]{1,0:T(8,128)(2,1)S(1)}, u32[]{:S(2)}, u32[]{:S(2)}) collective-permute-start(bf16[128,1024]{1,0:T(8,128)(2,1)S(1)} %shard_map.79.refs_0_), channel_id=1, source_target_pairs={{0,96},{1,97},{2,98},{3,99},{4,100},{5,101},{6,102},{7,103},{8,104... | collective-permute-start | bytes 786440 | tf_op jit(solution)/shard_map/x1/ppermute | solution.py:114
  17.7 4.6 %collective-permute-start.12 = (bf16[64,768]{1,0:T(8,128)(2,1)S(1)}, bf16[64,768]{1,0:T(8,128)(2,1)S(1)}, u32[]{:S(2)}, u32[]{:S(2)}) collective-permute-start(bf16[64,768]{1,0:T(8,128)(2,1)S(1)} %collective-permute-done.2.refs_1_.refs_0_.refs_2_), channel_id=1, source_target_pairs={{0,1},{1,0},{2,3},{3,2},{4,5},{5,4},{6,7},{7,6},{8,9},{9,8},{10,11... | collective-permute-start | bytes 294920 | tf_op jit(solution)/shard_map/low_far/ppermute | solution.py:114
  18.4 10.4 %collective-permute-start.15 = (bf16[128,1024]{1,0:T(8,128)(2,1)S(1)}, bf16[128,1024]{1,0:T(8,128)(2,1)S(1)}, u32[]{:S(2)}, u32[]{:S(2)}) collective-permute-start(bf16[128,1024]{1,0:T(8,128)(2,1)S(1)} %shard_map.79.refs_0_), channel_id=1, source_target_pairs={{0,64},{1,65},{2,66},{3,67},{4,68},{5,69},{6,70},{7,71},{8,72},{9,... | collective-permute-start | bytes 786440 | tf_op jit(solution)/shard_map/x2/ppermute | solution.py:114
  22.3 10.9 %copy-start.4 = (bf16[768,64]{0,1:T(8,128)(2,1)S(1)}, bf16[768,64]{0,1:T(8,128)(2,1)}, u32[]{:S(2)}) copy-start(bf16[768,64]{0,1:T(8,128)(2,1)} %param.6) | copy-start | bytes 294916
  22.3 10.9 %collective-permute-start.13 = (bf16[128,768]{1,0:T(8,128)(2,1)S(1)}, bf16[128,768]{1,0:T(8,128)(2,1)S(1)}, u32[]{:S(2)}, u32[]{:S(2)}) collective-permute-start(bf16[128,768]{1,0:T(8,128)(2,1)S(1)} %shard_map.80), channel_id=1, source_target_pairs={{0,14},{1,15},{2,0},{3,1},{4,2},{5,3},{6,4},{7,5},{8,6},{9,7},{10,... | collective-permute-start | bytes 589832 | tf_op jit(solution)/shard_map/lup/ppermute | solution.py:114
  24.6 5.4 %collective-permute-start.9 = (bf16[128,1024]{1,0:T(8,128)(2,1)S(1)}, bf16[128,1024]{1,0:T(8,128)(2,1)S(1)}, u32[]{:S(2)}, u32[]{:S(2)}) collective-permute-start(bf16[128,1024]{1,0:T(8,128)(2,1)S(1)} %collective-permute-done.8.refs_2_), channel_id=1, source_target_pairs={{0,16},{1,17},{2,18},{3,19},{4,20},{5,21},{6,22},{7,23},{8,24},{9,... | collective-permute-start | bytes 786440 | tf_op jit(solution)/shard_map/c2/ppermute | solution.py:114
  27.0 3.3 %collective-permute-start.7 = (bf16[128,1024]{1,0:T(8,128)(2,1)S(1)}, bf16[128,1024]{1,0:T(8,128)(2,1)S(1)}, u32[]{:S(2)}, u32[]{:S(2)}) collective-permute-start(bf16[128,1024]{1,0:T(8,128)(2,1)S(1)} %collective-permute-done.6.refs_1_), channel_id=1, source_target_pairs={{0,16},{1,17},{2,18},{3,19},{4,20},{5,21},{6,22},{7,23},{8,24},{9,... | collective-permute-start | bytes 786440 | tf_op jit(solution)/shard_map/c1/ppermute | solution.py:114
  27.1 7.3 %collective-permute-start.14 = (bf16[128,768]{1,0:T(8,128)(2,1)S(1)}, bf16[128,768]{1,0:T(8,128)(2,1)S(1)}, u32[]{:S(2)}, u32[]{:S(2)}) collective-permute-start(bf16[128,768]{1,0:T(8,128)(2,1)S(1)} %shard_map.81), channel_id=1, source_target_pairs={{0,2},{1,3},{2,4},{3,5},{4,6},{5,7},{6,8},{7,9},{8,10},{9,11},{10,... | collective-permute-start | bytes 589832 | tf_op jit(solution)/shard_map/ldn/ppermute | solution.py:114
  28.8 9.0 %copy-start = (bf16[1024,1024]{1,0:T(8,128)(2,1)S(1)}, bf16[1024,1024]{1,0:T(8,128)(2,1)}, u32[]{:S(2)}) copy-start(bf16[1024,1024]{1,0:T(8,128)(2,1)} %refs_8_.1) | copy-start | bytes 6291460
  28.8 11.3 %collective-permute-start.3 = (bf16[128,768]{1,0:T(8,128)(2,1)S(1)}, bf16[128,768]{1,0:T(8,128)(2,1)S(1)}, u32[]{:S(2)}, u32[]{:S(2)}) collective-permute-start(bf16[128,768]{1,0:T(8,128)(2,1)S(1)} %shard_map.77), channel_id=1, source_target_pairs={{0,14},{1,15},{2,0},{3,1},{4,2},{5,3},{6,4},{7,5},{8,6},{9,7},{10,... | collective-permute-start | bytes 589832 | tf_op jit(solution)/shard_map/up/ppermute | solution.py:114
  30.0 10.1 %collective-permute-start.4 = (bf16[128,768]{1,0:T(8,128)(2,1)S(1)}, bf16[128,768]{1,0:T(8,128)(2,1)S(1)}, u32[]{:S(2)}, u32[]{:S(2)}) collective-permute-start(bf16[128,768]{1,0:T(8,128)(2,1)S(1)} %shard_map.78), channel_id=1, source_target_pairs={{0,2},{1,3},{2,4},{3,5},{4,6},{5,7},{6,8},{7,9},{8,10},{9,11},{10,... | collective-permute-start | bytes 589832 | tf_op jit(solution)/shard_map/down/ppermute | solution.py:114
  30.3 6.3 %collective-permute-start.17 = (bf16[128,1024]{1,0:T(8,128)(2,1)S(1)}, bf16[128,1024]{1,0:T(8,128)(2,1)S(1)}, u32[]{:S(2)}, u32[]{:S(2)}) collective-permute-start(bf16[128,1024]{1,0:T(8,128)(2,1)S(1)} %collective-permute-done.15.refs_3_), channel_id=1, source_target_pairs={{0,16},{1,17},{2,18},{3,19},{4,20},{5,21},{6,22},{7,23},{8,24},{9,... | collective-permute-start | bytes 786440 | tf_op jit(solution)/shard_map/c3/ppermute | solution.py:114
  33.2 6.9 %collective-permute-start.10 = (bf16[64,768]{1,0:T(8,128)(2,1)S(1)}, bf16[64,768]{1,0:T(8,128)(2,1)S(1)}, u32[]{:S(2)}, u32[]{:S(2)}) collective-permute-start(bf16[64,768]{1,0:T(8,128)(2,1)S(1)} %bitcast.5), channel_id=1, source_target_pairs={{0,1},{1,0},{2,3},{3,2},{4,5},{5,4},{6,7},{7,6},{8,9},{9,8},{10,11... | collective-permute-start | bytes 294920 | tf_op jit(solution)/shard_map/low_own/ppermute | solution.py:114
  34.5 3.3 %collective-permute-start.16 = (bf16[128,1024]{1,0:T(8,128)(2,1)S(1)}, bf16[128,1024]{1,0:T(8,128)(2,1)S(1)}, u32[]{:S(2)}, u32[]{:S(2)}) collective-permute-start(bf16[128,1024]{1,0:T(8,128)(2,1)S(1)} %shard_map.79.refs_0_), channel_id=1, source_target_pairs={{0,16},{1,17},{2,18},{3,19},{4,20},{5,21},{6,22},{7,23},{8,24},{9,... | collective-permute-start | bytes 786440 | tf_op jit(solution)/shard_map/c0/ppermute | solution.py:114
  36.6 3.5 %copy-start.2 = (bf16[1024,1024]{1,0:T(8,128)(2,1)S(1)}, bf16[1024,1024]{1,0:T(8,128)(2,1)}, u32[]{:S(2)}) copy-start(bf16[1024,1024]{1,0:T(8,128)(2,1)} %refs_9_.1) | copy-start | bytes 6291460
  36.6 3.5 %copy-start.1 = (f32[768,1024]{1,0:T(8,128)S(1)}, f32[768,1024]{1,0:T(8,128)}, u32[]{:S(2)}) copy-start(f32[768,1024]{1,0:T(8,128)} %refs_11_.1) | copy-start | bytes 9437188
